TPU v7x, 256 devices: a whole 4x4x8 slice. The times are simulated.
256 devices in a mesh: track: 4 (over x_hi, core), tile: 64 (over z, y, x_lo).
Axes of the slice: x: 4 (x_hi: 2, x_lo: 2; x = x_hi * 2 + x_lo), y: 4, z: 8, core: 2. Of those that a mesh axis runs over, the one named last changes fastest.
Arguments:
- displacement: float32 [4, 5120, 1024], P('track', 'tile'), may hold values from -6 to 6
- velocity: float32 [4, 5120, 1024], P('track', 'tile'), may hold values from -3 to 3
- seasonal: float32 [2, 4, 5120, 1024], P(None, 'track', 'tile'), may hold values from -3 to 3
- cov_diag: float32 [4, 4, 5120, 1024], P(None, 'track', 'tile'), may hold values from 0.05 to 1
- cov_corr: float32 [6, 4, 5120, 1024], P(None, 'track', 'tile'), may hold values from -0.3 to 0.3
- observed: float32 [4, 5120, 1024], P('track', 'tile'), may hold values from -9 to 9
- noise_var: float32 [4, 5120, 1024], P('track', 'tile'), may hold values from 0.1 to 1
- coherence: float32 [4, 5120, 1024], P('track', 'tile'), may hold values from 0.2 to 1
- valid: int32 [4, 5120, 1024], P('track', 'tile'), may hold values 0 or 1
- screen_operator: bfloat16 [4, 5120, 5120], P('track', None, 'tile'), may hold values from -0.25 to 0.25
- process_noise: float32 [4], replicated, may hold values from 0.05 to 0.5
- track_scene: int32 [4], P('track'), may hold values from 0 to 15
- scene_interval: float32 [16], replicated, may hold values from 0.5 to 2
- margin_up: int32 [4, 64, 40], P('track', 'tile'), may hold values from -1 to 639, as said below
- margin_down: int32 [4, 64, 40], P('track', 'tile'), may hold values from -1 to 632, as said below
Outputs:
- new_state: float32 [4, 4, 5120, 1024], P(None, 'track', 'tile')
- new_cov: float32 [10, 4, 5120, 1024], P(None, 'track', 'tile')
Inputs may be any that keep to these rules, and one draw needn't show every extreme that they name: Slot j of margin_up at track t and tile k and slot j of margin_down at track t + 1 and tile k name blocks of the same ground; one is -1 (empty) exactly where the other is. margin_up names blocks of the last 128 columns, margin_down of the first 128; non-empty entries of one list are distinct; the last track's margin_up and the first track's margin_down are empty; for every pair of tracks some tile has all 40 slots filled. `margin_down`: see margin_up.
All inputs are finite; a program needn't handle non-finite values. No bound on the sum of `valid` on one device may be relied on, other than what follows from the above.
Results may differ from a plain program's by a relative error of at most 0.0014.
Values may be sent and summed in bfloat16 or wider, within the bound.
No kernel may reach another device: no remote copies, remote signals or barrier semaphores. Data moves between devices by JAX's collectives and lax.ppermute only.
A program may use at most 64 MiB of HBM per device.

v0:
```python
from functools import reduce
import math

import jax
import jax.numpy as jnp
from jax import lax
from jax.sharding import PartitionSpec as P

SEASON_RATE = 2.0 * math.pi * 12.0 / 365.25
ALONG_COEF = 0.2
ACROSS_COEF = 0.1
WEIGHT_FLOOR = 0.1
BLOCK_SCALE = 0.25
PAIR_LIST = ((0, 1), (0, 2), (0, 3), (1, 2), (1, 3), (2, 3))


def in_blocks(array, dim, size):
    shape = array.shape
    blocks = array.reshape(*shape[:dim], size, shape[dim] // size, *shape[dim + 1 :])
    return jnp.moveaxis(blocks, dim, 0)


def sent_and_summed(array, axis, dim):
    blocks = in_blocks(array, dim, lax.axis_size(axis))
    arrived = lax.all_to_all(blocks, axis, split_axis=0, concat_axis=0, tiled=True)
    return arrived.sum(axis=0)


def extended(cells, sides, width):
    for axis, dim in sides:
        count = lax.axis_size(axis)
        ends = count - 1
        head = lax.slice_in_dim(cells, 0, width, axis=dim)
        tail = lax.slice_in_dim(cells, cells.shape[dim] - width, cells.shape[dim], axis=dim)
        cells = jnp.concatenate(
            [
                lax.ppermute(tail, axis, [(i, (i + 1) % count) for i in range(ends)]),
                cells,
                lax.ppermute(head, axis, [((i + 1) % count, i) for i in range(ends)]),
            ],
            axis=dim,
        )
    return cells


def from_behind(value, axis, steps):
    count = lax.axis_size(axis)
    leading, last = (max(0, -steps), min(count, count - steps))
    return lax.ppermute(value, axis, [(source, source + steps) for source in range(leading, last)])


def add_all(items):
    return reduce(lambda a, b: a + b, items)


def predict(state_now, cov_diag, cov_corr, interval, process_noise):
    deviation = [jnp.sqrt(cov_diag[i]) for i in range(4)]
    covariance = [[None] * 4 for i in range(4)]
    for i in range(4):
        covariance[i][i] = cov_diag[i]
    for n, (i, j) in enumerate(PAIR_LIST):
        covariance[i][j] = cov_corr[n] * deviation[i] * deviation[j]
        covariance[j][i] = covariance[i][j]
    rotate_cos = jnp.cos(SEASON_RATE * interval)
    rotate_sin = jnp.sin(SEASON_RATE * interval)
    transition = [
        [1.0, interval, None, None],
        [None, 1.0, None, None],
        [None, None, rotate_cos, -rotate_sin],
        [None, None, rotate_sin, rotate_cos],
    ]
    state_pred = [
        add_all([transition[i][k] * state_now[k] for k in range(4) if transition[i][k] is not None])
        for i in range(4)
    ]
    left_product = [
        [
            add_all(
                [
                    transition[i][k] * covariance[k][j]
                    for k in range(4)
                    if transition[i][k] is not None
                ]
            )
            for j in range(4)
        ]
        for i in range(4)
    ]
    pred_cov = [
        [
            add_all(
                [
                    left_product[i][k] * transition[j][k]
                    for k in range(4)
                    if transition[j][k] is not None
                ]
            )
            for j in range(4)
        ]
        for i in range(4)
    ]
    for i in range(4):
        pred_cov[i][i] = pred_cov[i][i] + process_noise[i] * interval
    return (state_pred, pred_cov)


def update(state_pred, pred_cov, innovation, noise_var, coherence, valid_mask):
    cross_cov = [pred_cov[i][0] + pred_cov[i][2] for i in range(4)]
    variance = cross_cov[0] + cross_cov[2] + noise_var / coherence
    new_state = [
        state_pred[i] + valid_mask * (cross_cov[i] / variance) * innovation for i in range(4)
    ]
    diag_out = [
        pred_cov[i][i] - valid_mask * cross_cov[i] * cross_cov[i] / variance for i in range(4)
    ]
    pair_out = [
        pred_cov[i][j] - valid_mask * cross_cov[i] * cross_cov[j] / variance for i, j in PAIR_LIST
    ]
    return (jnp.stack(new_state), jnp.stack(diag_out + pair_out))


def pick_one(block_data, index_list):
    safe_index = jnp.where(index_list >= 0, index_list, 0)
    keep_mask = (index_list >= 0).astype(jnp.float32)
    return block_data[:, safe_index] * keep_mask[None, :, None]


def place_one(index_list, row_data, block_count):
    safe_index = jnp.where(index_list >= 0, index_list, block_count)
    blank = jnp.zeros((row_data.shape[0], block_count, row_data.shape[2]), jnp.float32)
    return blank.at[:, safe_index].add(row_data, mode="drop")


def local(
    displacement,
    velocity,
    seasonal,
    cov_diag,
    cov_corr,
    observed,
    noise_var,
    coherence,
    valid,
    screen_operator,
    process_noise,
    track_scene,
    scene_interval,
    margin_up,
    margin_down,
):
    table_size = scene_interval.shape[0]
    onehot = (jnp.arange(table_size) == track_scene[0]).astype(jnp.float32)
    interval = jnp.sum(onehot * scene_interval)
    state_now = [displacement, velocity, seasonal[0], seasonal[1]]
    state_pred, pred_cov = predict(state_now, cov_diag, cov_corr, interval, process_noise)
    valid_mask = valid.astype(jnp.float32)
    weight = coherence * valid_mask
    innovation_raw = observed - (state_pred[0] + state_pred[2])
    row_count = innovation_raw.shape[1]
    col_count = innovation_raw.shape[2]
    block_table = (
        jnp.arange(col_count)[:, None] // 32 == jnp.arange(col_count // 32)[None, :]
    ).astype(jnp.float32)
    weighted = (weight * innovation_raw)[0]
    block_sums = (
        jnp.dot(
            weighted,
            block_table,
            precision=lax.Precision.HIGHEST,
            preferred_element_type=jnp.float32,
        )
        * BLOCK_SCALE
    ).astype(jnp.bfloat16)
    operator_cols = screen_operator[0]
    screen = sent_and_summed(
        jnp.dot(operator_cols, block_sums, preferred_element_type=jnp.float32), "tile", 0
    )
    spread = jnp.dot(
        screen, block_table.T, precision=lax.Precision.HIGHEST, preferred_element_type=jnp.float32
    )
    cleaned = innovation_raw - spread[None]
    padded_rows = extended(cleaned.astype(jnp.bfloat16), (("tile", 1),), 1).astype(cleaned.dtype)
    zero_column = jnp.zeros((1, row_count, 1), jnp.float32)
    left_cells = jnp.concatenate([zero_column, cleaned[:, :, :-1]], axis=2)
    right_cells = jnp.concatenate([cleaned[:, :, 1:], zero_column], axis=2)
    smooth = (
        cleaned
        + ALONG_COEF * (padded_rows[:, :-2] + padded_rows[:, 2:] - 2.0 * cleaned)
        + ACROSS_COEF * (left_cells + right_cells - 2.0 * cleaned)
    )
    block_count = row_count * (col_count // 128)
    payload = jnp.stack(
        [(weight * smooth).reshape(block_count, 128), weight.reshape(block_count, 128)]
    )
    upward = pick_one(payload, margin_up[0, 0])
    downward = pick_one(payload, margin_down[0, 0])
    from_below = from_behind(upward.astype(jnp.bfloat16), "track", 1).astype(upward.dtype)
    from_above = from_behind(downward.astype(jnp.bfloat16), "track", -1).astype(downward.dtype)
    received = place_one(margin_down[0, 0], from_below, block_count) + place_one(
        margin_up[0, 0], from_above, block_count
    )
    received_wv = received[0].reshape(1, row_count, col_count)
    received_w = received[1].reshape(1, row_count, col_count)
    innovation = ((weight + WEIGHT_FLOOR) * smooth + received_wv) / (
        weight + WEIGHT_FLOOR + received_w
    )
    return update(state_pred, pred_cov, innovation, noise_var, coherence, valid_mask)


def solution(mesh):
    in_specs = (
        P("track", "tile", None),
        P("track", "tile", None),
        P(None, "track", "tile", None),
        P(None, "track", "tile", None),
        P(None, "track", "tile", None),
        P("track", "tile", None),
        P("track", "tile", None),
        P("track", "tile", None),
        P("track", "tile", None),
        P("track", None, "tile"),
        P(),
        P("track"),
        P(),
        P("track", "tile", None),
        P("track", "tile", None),
    )
    out_specs = (P(None, "track", "tile", None), P(None, "track", "tile", None))
    return jax.shard_map(local, mesh=mesh, in_specs=in_specs, out_specs=out_specs, check_vma=False)
```

profile of v0, /device:TPU:27, one launch (start us, length us, event | category | flops | bytes accessed | tf_op | source)
XLA Modules:
  0.0 112.9 jit_solution(5340820187979511994)
XLA Ops:
  0.6 0.0 copy-start
  1.4 1.3 %fusion.29 = f32[]{:T(128)} fusion(f32[16]{0:T(128)} %param.27, s32[]{:T(128)} %bitcast.194), kind=kLoop, calls=%fused_computation.110 | loop fusion | flops 47 | bytes 72 | tf_op jit(solution)/shard_map/reduce_sum | solution.py:153
  3.6 1.4 %fusion.42 = (f32[1]{0:T(128)}, f32[1]{0:T(128)}, f32[1]{0:T(128)}, f32[1]{0:T(128)}) fusion(f32[4]{0:T(128)} %param.25), kind=kLoop, calls=%fused_computation.119 | loop fusion | bytes 32 | tf_op jit(solution)/shard_map/slice | solution.py:103
  6.4 1.1 convert_multiply_fusion.3
  7.5 3.6 %fusion.19 = (f32[1,80,1024]{2,1,0:T(8,128)}, f32[1,80,1024]{2,1,0:T(8,128)}, f32[1,80,1024]{2,1,0:T(8,128)S(1)}) fusion(f32[4,1,80,1024]{3,2,1,0:T(8,128)} %param.18, f32[]{:T(128)S(6)} %mul.1267, f32[]{:T(128)} %fusion.29, f32[6,1,80,1024]{3,2,1,0:T(8,128)} %param.19, f32[1,80,1024]{2,1,0:T(8,128)} %param.20, f32[2,1,80,1024]{3,2,1,0:T(8,128)} %param.17, ...), kind=kLoop, calls=%fused_computation.61 | loop fusion | flops 1310720 | bytes 3605516 | tf_op jit(solution)/shard_map/add | solution.py:103
  11.1 0.7 fusion.1
  11.8 0.0 copy-done.5
  11.8 0.3 convolution_bitcast_fusion
  12.1 0.0 copy-start.25
  12.1 0.0 copy-start.26
  12.1 0.0 copy-start.1
  12.1 0.0 copy-start.2
  12.1 1.5 %reshape.1097 = f32[64,80,32]{1,0,2:T(8,128)} reshape(f32[5120,32]{0,1:T(8,128)S(1)} %convolution_bitcast_fusion) | data formatting | bytes 1310720 | tf_op jit(solution)/shard_map/reshape | solution.py:19
  13.6 2.8 %copy.19 = f32[64,80,32]{1,2,0:T(8,128)} copy(f32[64,80,32]{1,0,2:T(8,128)} %reshape.1097) | data formatting | bytes 1310720 | tf_op jit(solution)/shard_map/reshape | solution.py:19
  16.4 0.0 copy-done.19
  16.4 12.4 %all-to-all-start = ((f32[64,80,32]{1,2,0:T(8,128)}), f32[64,80,32]{1,2,0:T(8,128)}, u32[]{:S(2)}, u32[]{:S(2)}) async-start(f32[64,80,32]{1,2,0:T(8,128)} %copy.19), calls=%async_computation | async-start | bytes 2097152 | tf_op jit(solution)/shard_map/all_to_all | solution.py:25
  28.8 0.0 copy-done.25
  28.9 0.0 copy-done.26
  32.8 3.2 %bitcast_dynamic-update-slice_fusion.8 = (f32[10,1,80,1024]{3,2,1,0:T(8,128)S(1)}, f32[1,80,1024]{2,1,0:T(8,128)S(1)}, f32[1,80,1024]{2,1,0:T(8,128)S(1)}, f32[1...) fusion(f32[1,80,1024]{2,1,0:T(8,128)} %get-tuple-element.22, ...), kind=kLoop, calls=%fused_computation.33 | loop fusion | flops 3686399 | bytes 8194564
  36.0 0.0 copy-start.10
  36.1 0.0 copy-start.12
  36.1 0.0 copy-start.15
  36.1 0.0 copy-start.17
  36.1 0.0 copy-start.18
  36.1 0.8 bitcast_dynamic-update-slice_fusion.7
  37.0 0.1 bitcast_dynamic-update-slice_fusion.6
  37.1 1.7 %fusion.6 = (f32[10,1,80,1024]{3,2,1,0:T(8,128)S(1)}, f32[1,80,1024]{2,1,0:T(8,128)}) fusion(f32[10,1,80,1024]{3,2,1,0:T(8,128)S(1)} %bitcast_dynamic-update-slice_fusion.6, f32[1,80,1024]{2,1,0:T(8,128)S(1)} %get-tuple-element.9, s32[1,80,1024]{2,1,0:T(8,128)S(1)} %copy-done.1, f32[]{:T(128)S(6)} %mul.1350, f32[]{:T(128)S(6)} %sin.3, f32[]{:T(128)S(6)} %cos.3, ...), kind=kLoop, calls=%fused_computation.16 | loop fusion | flops 2211840 | bytes 3607556
  38.8 0.9 bitcast_dynamic-update-slice_fusion.5
  39.7 0.1 bitcast_dynamic-update-slice_fusion.4
  39.8 0.0 copy-start.24
  39.8 1.7 %copy-done.24 = f32[10,1,80,1024]{3,2,1,0:T(8,128)} copy-done((f32[10,1,80,1024]{3,2,1,0:T(8,128)}, f32[10,1,80,1024]{3,2,1,0:T(8,128)S(1)}, u32[]{:S(2)}) %copy-start.24) | copy-done | bytes 3276824
  41.6 1.8 %stack_reshape.7 = f32[1,640,128]{2,1,0:T(8,128)} reshape(f32[1,80,1024]{2,1,0:T(8,128)} %copy-done.5) | data formatting | bytes 655360 | tf_op jit(solution)/shard_map/stack;reshape | solution.py:192
  43.3 3.1 %bitcast_dynamic-update-slice_fusion.3 = f32[10,1,80,1024]{3,2,1,0:T(8,128)} fusion(f32[10,1,80,1024]{3,2,1,0:T(8,128)} %copy-done.24, f32[1,80,1024]{2,1,0:T(8,128)S(1)} %get-tuple-element.9, f32[1,80,1024]{2,1,0:T(8,128)} %get-tuple-element.5, f32[1,80,1024]{2,1,0:T(8,128)S(1)} %get-tuple-element.13, s32[1,80,1024]{2,1,0:T(8,128)S(1)} %copy-done.1, ...), kind=kLoop, calls=%fused_computation.27 | loop fusion | flops 983040 | bytes 2949640
  46.5 1.9 %bitcast_dynamic-update-slice_fusion.2 = f32[10,1,80,1024]{3,2,1,0:T(8,128)} fusion(f32[10,1,80,1024]{3,2,1,0:T(8,128)} %bitcast_dynamic-update-slice_fusion.3, f32[1,80,1024]{2,1,0:T(8,128)} %copy-done.21, f32[1,80,1024]{2,1,0:T(8,128)S(1)} %get-tuple-element.9, f32[1,80,1024]{2,1,0:T(8,128)S(1)} %get-tuple-element.10, f32[1,80,1024]{2,1,0:T(8,128)} %copy-done.7, ...), kind=kLoop, calls=%fused_computation.26 | loop fusion | flops 409600 | bytes 1966080
  48.4 0.9 bitcast_dynamic-update-slice_fusion.1
  49.3 0.9 bitcast_dynamic-update-slice_fusion
  50.2 5.3 %all-to-all-done = f32[64,80,32]{1,2,0:T(8,128)} async-done(((f32[64,80,32]{1,2,0:T(8,128)}), f32[64,80,32]{1,2,0:T(8,128)}, u32[]{:S(2)}, u32[]{:S(2)}) %all-to-all-start) | async-done | bytes 655392 | tf_op jit(solution)/shard_map/all_to_all | solution.py:25
  55.5 1.3 %reduce_sum.19 = f32[80,32]{0,1:T(8,128)S(1)} reduce(f32[64,80,32]{1,2,0:T(8,128)} %all-to-all-done, f32[]{:T(128)} %constant.12.clone.1), dimensions={0}, to_apply=%region_1.2 | reduce | flops 161280 | bytes 665604 | tf_op jit(solution)/shard_map/reduce_sum | solution.py:26
  56.9 1.6 %fusion.43 = (bf16[1,80,1024]{2,1,0:T(8,128)(2,1)S(1)}, f32[1,80,1024]{2,1,0:T(8,128)S(1)}) fusion(f32[1,80,1024]{2,1,0:T(8,128)} %copy-done.19, f32[80,32]{0,1:T(8,128)S(1)} %reduce_sum.19, s32[1024]{0:T(1024)S(1)} %add_select_fusion), kind=kOutput, calls=%fused_computation.120 | convolution fusion | flops 31653888 | bytes 833536 | tf_op jit(solution)/shard_map/dot_general | solution.py:178
  58.5 3.0 %collective-permute-start = (bf16[1,1,1024]{2,1,0:T(2,128)(2,1)S(1)}, bf16[1,1,1024]{2,1,0:T(2,128)(2,1)S(1)}, u32[]{:S(2)}, u32[]{:S(2)}) collective-permute-start(bf16[1,1,1024]{2,1,0:T(2,128)(2,1)S(1)} %get-tuple-element.31), channel_id=1, source_target_pairs={{0,1},{1,2},{2,3},{3,4},{4,5},{5,6},{6,7},{7,8},{8,9},{9,10},{10,1... | collective-permute-start | bytes 6152 | tf_op jit(solution)/shard_map/ppermute | solution.py:37
  61.5 2.3 %collective-permute-start.1 = (bf16[1,1,1024]{2,1,0:T(2,128)(2,1)S(1)}, bf16[1,1,1024]{2,1,0:T(2,128)(2,1)S(1)}, u32[]{:S(2)}, u32[]{:S(2)}) collective-permute-start(bf16[1,1,1024]{2,1,0:T(2,128)(2,1)S(1)} %get-tuple-element.32), channel_id=1, source_target_pairs={{1,0},{2,1},{3,2},{4,3},{5,4},{6,5},{7,6},{8,7},{9,8},{10,9},{11,1... | collective-permute-start | bytes 6152 | tf_op jit(solution)/shard_map/ppermute | solution.py:39
  63.8 0.2 fusion.40
  63.9 0.0 collective-permute-done
  63.9 4.9 %collective-permute-done.1 = bf16[1,1,1024]{2,1,0:T(2,128)(2,1)S(1)} collective-permute-done((bf16[1,1,1024]{2,1,0:T(2,128)(2,1)S(1)}, bf16[1,1,1024]{2,1,0:T(2,128)(2,1)S(1)}, u32[]{:S(2)}, u32[]{:S(2)}) %collective-permute-start.1) | collective-permute-done | bytes 2080 | tf_op jit(solution)/shard_map/ppermute | solution.py:39
  68.9 0.9 fusion.38
  69.8 0.8 stack_reshape.6
  70.6 2.4 %pad_maximum_fusion.1 = f32[2,640,128]{2,0,1:T(2,128)} fusion(f32[1,640,128]{2,0,1:T(1,128)S(1)} %bitcast.195, f32[1,640,128]{2,0,1:T(1,128)} %bitcast.196), kind=kLoop, calls=%fused_computation.10 | loop fusion | flops 163840 | bytes 1310720 | tf_op jit(solution)/shard_map/stack | solution.py:192
  73.0 1.7 %gather_fusion = f32[40,2,128]{2,1,0:T(2,128)S(1)} fusion(f32[2,640,128]{2,0,1:T(2,128)} %pad_maximum_fusion.1, s32[1024]{0:T(1024)S(1)} %pad_clamp_fusion.1), kind=kCustom, calls=%fused_computation | custom fusion | bytes 82080 | tf_op jit(solution)/shard_map/gather | solution.py:125
  74.7 0.1 fusion.24
  74.8 8.4 %collective-permute-start.2 = (bf16[2,40,128]{2,0,1:T(2,128)(2,1)S(1)}, bf16[2,40,128]{2,0,1:T(2,128)(2,1)S(1)}, u32[]{:S(2)}, u32[]{:S(2)}) collective-permute-start(bf16[2,40,128]{2,0,1:T(2,128)(2,1)S(1)} %fusion.24), channel_id=1, source_target_pairs={{0,64},{64,128},{128,192},{1,65},{65,129},{129,193},{2,66},{66,130... | collective-permute-start | bytes 61448 | tf_op jit(solution)/shard_map/ppermute | solution.py:49
  83.2 1.7 %gather_fusion.1 = f32[40,2,128]{2,1,0:T(2,128)S(1)} fusion(f32[2,640,128]{2,0,1:T(2,128)} %pad_maximum_fusion.1, s32[1024]{0:T(1024)S(1)} %pad_clamp_fusion), kind=kCustom, calls=%fused_computation.1 | custom fusion | bytes 82080 | tf_op jit(solution)/shard_map/gather | solution.py:125
  84.9 0.1 fusion.25
  85.0 2.1 %collective-permute-start.3 = (bf16[2,40,128]{2,0,1:T(2,128)(2,1)S(1)}, bf16[2,40,128]{2,0,1:T(2,128)(2,1)S(1)}, u32[]{:S(2)}, u32[]{:S(2)}) collective-permute-start(bf16[2,40,128]{2,0,1:T(2,128)(2,1)S(1)} %fusion.25), channel_id=1, source_target_pairs={{64,0},{128,64},{192,128},{65,1},{129,65},{193,129},{66,2},{130,66... | collective-permute-start | bytes 61448 | tf_op jit(solution)/shard_map/ppermute | solution.py:49
  87.1 0.1 add_bitcast_fusion.2
  87.2 0.0 collective-permute-done.2
  87.2 4.4 %collective-permute-done.3 = bf16[2,40,128]{2,0,1:T(2,128)(2,1)S(1)} collective-permute-done((bf16[2,40,128]{2,0,1:T(2,128)(2,1)S(1)}, bf16[2,40,128]{2,0,1:T(2,128)(2,1)S(1)}, u32[]{:S(2)}, u32[]{:S(2)}) %collective-permute-start.3) | collective-permute-done | bytes 20512 | tf_op jit(solution)/shard_map/ppermute | solution.py:49
  91.7 1.0 broadcast.745
  92.7 8.8 %scatter_fusion = f32[2,640,128]{2,0,1:T(2,128)} fusion(f32[2,640,128]{2,0,1:T(2,128)} %broadcast.745, s32[80]{0:T(128)S(1)} %add_bitcast_fusion.2, f32[80,2,128]{2,1,0:T(2,128)S(1)} %convert_bitcast_fusion), kind=kCustom, calls=%fused_computation.2 | custom fusion | flops 20480 | bytes 246080 | tf_op jit(solution)/shard_map/add | solution.py:199
  101.6 4.0 %slice_reduce_fusion.1 = (f32[640,128]{1,0:T(8,128)}, f32[640,128]{1,0:T(8,128)}) fusion(f32[2,640,128]{2,0,1:T(2,128)} %scatter_fusion), kind=kLoop, calls=%fused_computation.18 | loop fusion | bytes 1310720 | tf_op jit(solution)/shard_map/slice | solution.py:202
  105.5 1.8 %reshape_squeeze.6 = f32[1,80,1024]{2,1,0:T(8,128)} reshape(f32[640,128]{1,0:T(8,128)} %get-tuple-element.2) | data formatting | bytes 655360 | tf_op jit(solution)/shard_map/reshape;squeeze | solution.py:202
  107.3 1.8 %reshape_squeeze.7 = f32[1,80,1024]{2,1,0:T(8,128)} reshape(f32[640,128]{1,0:T(8,128)} %get-tuple-element.3) | data formatting | bytes 655360 | tf_op jit(solution)/shard_map/reshape;squeeze | solution.py:203
  109.0 2.3 %add_bitcast_fusion.1 = (f32[1,1,80,1024]{3,2,1,0:T(8,128)S(1)}, f32[1,80,1024]{2,1,0:T(8,128)S(1)}) fusion(f32[1,80,1024]{2,1,0:T(8,128)S(1)} %get-tuple-element.13, f32[1,80,1024]{2,1,0:T(8,128)S(1)} %get-tuple-element.9, s32[1,80,1024]{2,1,0:T(8,128)S(1)} %copy-done.1, f32[1,80,1024]{2,1,0:T(8,128)} %param.15, f32[1,80,1024]{2,1,0:T(8,128)S(1)} %copy-done.14, ...), kind=kLoop, calls=%fused_computation.65 | loop fusion | flops 983040 | bytes 3604484 | tf_op jit(solution)/shard_map/stack | solution.py:119
  111.4 0.3 fusion.14
  111.7 1.2 %pad_maximum_fusion = f32[4,1,80,1024]{3,2,1,0:T(8,128)} fusion(f32[1,1,80,1024]{3,2,1,0:T(8,128)S(1)} %get-tuple-element.27, f32[1,1,80,1024]{3,2,1,0:T(8,128)S(1)} %get-tuple-element.26, f32[1,1,80,1024]{3,2,1,0:T(8,128)S(1)} %get-tuple-element.28, f32[1,1,80,1024]{3,2,1,0:T(8,128)S(1)} %get-tuple-element.20), kind=kLoop, calls=%fused_computation.4 | loop fusion | flops 983040 | bytes 2621440 | tf_op jit(solution)/shard_map/stack | solution.py:119
  (47 shorter events, 0.2 us)
Async XLA Ops:
  0.6 11.2 %copy-start = (bf16[1,5120,80]{1,2,0:T(8,128)(2,1)S(1)}, bf16[1,5120,80]{1,2,0:T(8,128)(2,1)}, u32[]{:S(2)}) copy-start(bf16[1,5120,80]{1,2,0:T(8,128)(2,1)} %param.24) | copy-start | bytes 2457604
  7.5 4.3 %copy-start.5 = (f32[1,80,1024]{2,1,0:T(8,128)}, f32[1,80,1024]{2,1,0:T(8,128)S(1)}, u32[]{:S(2)}) copy-start(f32[1,80,1024]{2,1,0:T(8,128)S(1)} %convert_multiply_fusion.3) | copy-start | bytes 983044
  11.1 5.4 %copy-start.19 = (f32[1,80,1024]{2,1,0:T(8,128)}, f32[1,80,1024]{2,1,0:T(8,128)S(1)}, u32[]{:S(2)}) copy-start(f32[1,80,1024]{2,1,0:T(8,128)S(1)} %get-tuple-element.43) | copy-start | bytes 983044
  12.1 16.8 %copy-start.25 = (s32[1,1,40]{2,1,0:T(1,128)S(1)}, s32[1,1,40]{2,1,0:T(1,128)}, u32[]{:S(2)}) copy-start(s32[1,1,40]{2,1,0:T(1,128)} %param.28) | copy-start | bytes 484
  12.1 16.8 %copy-start.26 = (s32[1,1,40]{2,1,0:T(1,128)S(1)}, s32[1,1,40]{2,1,0:T(1,128)}, u32[]{:S(2)}) copy-start(s32[1,1,40]{2,1,0:T(1,128)} %param.29) | copy-start | bytes 484
  12.1 20.7 %copy-start.1 = (s32[1,80,1024]{2,1,0:T(8,128)S(1)}, s32[1,80,1024]{2,1,0:T(8,128)}, u32[]{:S(2)}) copy-start(s32[1,80,1024]{2,1,0:T(8,128)} %param.23) | copy-start | bytes 983044
  12.1 20.7 %copy-start.2 = (f32[4,1,80,1024]{3,2,1,0:T(8,128)S(1)}, f32[4,1,80,1024]{3,2,1,0:T(8,128)}, u32[]{:S(2)}) copy-start(f32[4,1,80,1024]{3,2,1,0:T(8,128)} %param.18) | copy-start | bytes 3932164
  16.4 39.1 %all-to-all-start = ((f32[64,80,32]{1,2,0:T(8,128)}), f32[64,80,32]{1,2,0:T(8,128)}, u32[]{:S(2)}, u32[]{:S(2)}) async-start(f32[64,80,32]{1,2,0:T(8,128)} %copy.19), calls=%async_computation | async-start | bytes 2097152 | tf_op jit(solution)/shard_map/all_to_all | solution.py:25
  32.8 3.3 %copy-start.20 = (f32[1,80,1024]{2,1,0:T(8,128)S(1)}, f32[1,80,1024]{2,1,0:T(8,128)}, u32[]{:S(2)}) copy-start(f32[1,80,1024]{2,1,0:T(8,128)} %get-tuple-element.23) | copy-start | bytes 983044
  36.0 2.8 %copy-start.10 = (f32[1,80,1024]{2,1,0:T(8,128)}, f32[1,80,1024]{2,1,0:T(8,128)S(1)}, u32[]{:S(2)}) copy-start(f32[1,80,1024]{2,1,0:T(8,128)S(1)} %get-tuple-element.16) | copy-start | bytes 983044
  36.1 2.8 %copy-start.12 = (f32[1,80,1024]{2,1,0:T(8,128)}, f32[1,80,1024]{2,1,0:T(8,128)S(1)}, u32[]{:S(2)}) copy-start(f32[1,80,1024]{2,1,0:T(8,128)S(1)} %get-tuple-element.17) | copy-start | bytes 983044
  36.1 2.8 %copy-start.15 = (f32[1,80,1024]{2,1,0:T(8,128)}, f32[1,80,1024]{2,1,0:T(8,128)S(1)}, u32[]{:S(2)}) copy-start(f32[1,80,1024]{2,1,0:T(8,128)S(1)} %get-tuple-element.15) | copy-start | bytes 983044
  36.1 2.7 %copy-start.17 = (f32[1,80,1024]{2,1,0:T(8,128)}, f32[1,80,1024]{2,1,0:T(8,128)S(1)}, u32[]{:S(2)}) copy-start(f32[1,80,1024]{2,1,0:T(8,128)S(1)} %get-tuple-element.18) | copy-start | bytes 983044
  36.1 2.7 %copy-start.18 = (f32[1,80,1024]{2,1,0:T(8,128)}, f32[1,80,1024]{2,1,0:T(8,128)S(1)}, u32[]{:S(2)}) copy-start(f32[1,80,1024]{2,1,0:T(8,128)S(1)} %get-tuple-element.19) | copy-start | bytes 983044
  36.1 2.7 %copy-start.21 = (f32[1,80,1024]{2,1,0:T(8,128)}, f32[1,80,1024]{2,1,0:T(8,128)S(1)}, u32[]{:S(2)}) copy-start(f32[1,80,1024]{2,1,0:T(8,128)S(1)} %get-tuple-element.11) | copy-start | bytes 983044
  37.0 2.7 %copy-start.7 = (f32[1,80,1024]{2,1,0:T(8,128)}, f32[1,80,1024]{2,1,0:T(8,128)S(1)}, u32[]{:S(2)}) copy-start(f32[1,80,1024]{2,1,0:T(8,128)S(1)} %get-tuple-element.7) | copy-start | bytes 983044
  39.8 1.7 %copy-start.24 = (f32[10,1,80,1024]{3,2,1,0:T(8,128)}, f32[10,1,80,1024]{3,2,1,0:T(8,128)S(1)}, u32[]{:S(2)}) copy-start(f32[10,1,80,1024]{3,2,1,0:T(8,128)S(1)} %bitcast_dynamic-update-slice_fusion.4) | copy-start | bytes 9830404
  43.3 5.1 %copy-start.3 = (f32[1,80,1024]{2,1,0:T(8,128)S(1)}, f32[1,80,1024]{2,1,0:T(8,128)}, u32[]{:S(2)}) copy-start(f32[1,80,1024]{2,1,0:T(8,128)} %get-tuple-element.5) | copy-start | bytes 983044
  43.3 5.1 %copy-start.8 = (f32[1,80,1024]{2,1,0:T(8,128)S(1)}, f32[1,80,1024]{2,1,0:T(8,128)}, u32[]{:S(2)}) copy-start(f32[1,80,1024]{2,1,0:T(8,128)} %copy-done.7) | copy-start | bytes 983044
  43.3 5.1 %copy-start.11 = (f32[1,80,1024]{2,1,0:T(8,128)S(1)}, f32[1,80,1024]{2,1,0:T(8,128)}, u32[]{:S(2)}) copy-start(f32[1,80,1024]{2,1,0:T(8,128)} %copy-done.10) | copy-start | bytes 983044
  43.3 5.1 %copy-start.13 = (f32[1,80,1024]{2,1,0:T(8,128)S(1)}, f32[1,80,1024]{2,1,0:T(8,128)}, u32[]{:S(2)}) copy-start(f32[1,80,1024]{2,1,0:T(8,128)} %copy-done.12) | copy-start | bytes 983044
  43.3 6.0 %copy-start.16 = (f32[1,80,1024]{2,1,0:T(8,128)S(1)}, f32[1,80,1024]{2,1,0:T(8,128)}, u32[]{:S(2)}) copy-start(f32[1,80,1024]{2,1,0:T(8,128)} %copy-done.15) | copy-start | bytes 983044
  50.2 18.7 %copy-start.6 = (f32[1,80,1024]{2,1,0:T(8,128)S(1)}, f32[1,80,1024]{2,1,0:T(8,128)}, u32[]{:S(2)}) copy-start(f32[1,80,1024]{2,1,0:T(8,128)} %copy-done.5) | copy-start | bytes 983044
  50.2 20.4 %copy-start.23 = (f32[1,640,128]{2,1,0:T(8,128)S(1)}, f32[1,640,128]{2,1,0:T(8,128)}, u32[]{:S(2)}) copy-start(f32[1,640,128]{2,1,0:T(8,128)} %stack_reshape.7) | copy-start | bytes 983044
  58.5 5.5 %collective-permute-start = (bf16[1,1,1024]{2,1,0:T(2,128)(2,1)S(1)}, bf16[1,1,1024]{2,1,0:T(2,128)(2,1)S(1)}, u32[]{:S(2)}, u32[]{:S(2)}) collective-permute-start(bf16[1,1,1024]{2,1,0:T(2,128)(2,1)S(1)} %get-tuple-element.31), channel_id=1, source_target_pairs={{0,1},{1,2},{2,3},{3,4},{4,5},{5,6},{6,7},{7,8},{8,9},{9,10},{10,1... | collective-permute-start | bytes 6152 | tf_op jit(solution)/shard_map/ppermute | solution.py:37
  61.5 7.4 %collective-permute-start.1 = (bf16[1,1,1024]{2,1,0:T(2,128)(2,1)S(1)}, bf16[1,1,1024]{2,1,0:T(2,128)(2,1)S(1)}, u32[]{:S(2)}, u32[]{:S(2)}) collective-permute-start(bf16[1,1,1024]{2,1,0:T(2,128)(2,1)S(1)} %get-tuple-element.32), channel_id=1, source_target_pairs={{1,0},{2,1},{3,2},{4,3},{5,4},{6,5},{7,6},{8,7},{9,8},{10,9},{11,1... | collective-permute-start | bytes 6152 | tf_op jit(solution)/shard_map/ppermute | solution.py:39
  69.8 39.2 %copy-start.14 = (f32[1,80,1024]{2,1,0:T(8,128)S(1)}, f32[1,80,1024]{2,1,0:T(8,128)}, u32[]{:S(2)}) copy-start(f32[1,80,1024]{2,1,0:T(8,128)} %param.16) | copy-start | bytes 983044
  74.8 12.4 %collective-permute-start.2 = (bf16[2,40,128]{2,0,1:T(2,128)(2,1)S(1)}, bf16[2,40,128]{2,0,1:T(2,128)(2,1)S(1)}, u32[]{:S(2)}, u32[]{:S(2)}) collective-permute-start(bf16[2,40,128]{2,0,1:T(2,128)(2,1)S(1)} %fusion.24), channel_id=1, source_target_pairs={{0,64},{64,128},{128,192},{1,65},{65,129},{129,193},{2,66},{66,130... | collective-permute-start | bytes 61448 | tf_op jit(solution)/shard_map/ppermute | solution.py:49
  85.0 6.6 %collective-permute-start.3 = (bf16[2,40,128]{2,0,1:T(2,128)(2,1)S(1)}, bf16[2,40,128]{2,0,1:T(2,128)(2,1)S(1)}, u32[]{:S(2)}, u32[]{:S(2)}) collective-permute-start(bf16[2,40,128]{2,0,1:T(2,128)(2,1)S(1)} %fusion.25), channel_id=1, source_target_pairs={{64,0},{128,64},{192,128},{65,1},{129,65},{193,129},{66,2},{130,66... | collective-permute-start | bytes 61448 | tf_op jit(solution)/shard_map/ppermute | solution.py:49
  92.7 18.6 %copy-start.4 = (f32[1,80,1024]{2,1,0:T(8,128)S(1)}, f32[1,80,1024]{2,1,0:T(8,128)}, u32[]{:S(2)}) copy-start(f32[1,80,1024]{2,1,0:T(8,128)} %get-tuple-element.5) | copy-start | bytes 983044
  92.7 18.6 %copy-start.9 = (f32[1,80,1024]{2,1,0:T(8,128)S(1)}, f32[1,80,1024]{2,1,0:T(8,128)}, u32[]{:S(2)}) copy-start(f32[1,80,1024]{2,1,0:T(8,128)} %copy-done.7) | copy-start | bytes 983044
  109.0 2.3 %copy-start.22 = (f32[2,1,80,1024]{3,2,1,0:T(8,128)S(1)}, f32[2,1,80,1024]{3,2,1,0:T(8,128)}, u32[]{:S(2)}) copy-start(f32[2,1,80,1024]{3,2,1,0:T(8,128)} %param.17) | copy-start | bytes 1966084
where the time goes:
time: 114 us; the launch traced here: 113 us
  other arithmetic  37.5 us (33%)
  starting transfers between devices  28.2 us (25%)
  local copies, waits for them, and re-layouts  22.2 us (19%)
  waiting for transfers between devices  14.7 us (13%)
  between operations  7.86 us (7%)
  matrix products  2.54 us (2%)
    unnamed x9, other arithmetic  12.8 us
    all_to_all x1, starting transfers between devices, sent_and_summed(): lax.all_to_all(blocks, axis, split_axis=0, concat_axis=0, tiled=True)  12.4 us
    ppermute x2, starting transfers between devices, from_behind(): lax.ppermute(value, axis, [(source, source + steps) for source in range(l...  10.5 us
    add x1, other arithmetic, local(): place_one(margin_down[0, 0], from_below, block_count)  8.84 us
    all_to_all x1, waiting for transfers between devices, sent_and_summed(): lax.all_to_all(blocks, axis, split_axis=0, concat_axis=0, tiled=True)  5.29 us
    ppermute x1, waiting for transfers between devices, extended(): lax.ppermute(head, axis, [((i + 1) % count, i) for i in range(ends)])  4.94 us
    another operation x4, other arithmetic, update(): return (jnp.stack(new_state), jnp.stack(diag_out + pair_out))  4.78 us
    ppermute x2, waiting for transfers between devices, from_behind(): lax.ppermute(value, axis, [(source, source + steps) for source in range(l...  4.42 us
  transfers between devices with their start and end apart: 5, of which 3 were waited for; matrix products, arithmetic and copies ran while one was open for 16% of the time, Pallas kernels for 0%

commit v1 on v0

v1 whole, which is shorter than its diff:
```python
import functools
import math

import jax
import jax.numpy as jnp
from jax import lax
from jax.experimental import pallas as pl
from jax.experimental.pallas import tpu as pltpu
from jax.sharding import PartitionSpec as P

SEASON_RATE = 2.0 * math.pi * 12.0 / 365.25
ALONG_COEF = 0.2
ACROSS_COEF = 0.1
WEIGHT_FLOOR = 0.1
BLOCK_SCALE = 0.25
PAIR_LIST = ((0, 1), (0, 2), (0, 3), (1, 2), (1, 3), (2, 3))

R = 80
W = 1024
PAD = 8
WIN = R + 2 * PAD
SUB = WIN // 4
NB = 40
F32 = jnp.float32
BF16 = jnp.bfloat16

SMEM = pl.BlockSpec(memory_space=pltpu.SMEM)
VMEM = pl.BlockSpec(memory_space=pltpu.VMEM)
ANY = pl.BlockSpec(memory_space=pl.ANY)


def scene_terms(scene, table):
    interval = table[scene[0]]
    angle = jnp.full((1, 1), SEASON_RATE * interval, F32)
    return interval, jnp.cos(angle), jnp.sin(angle)


def front_kernel(
    tiles,
    scene,
    table,
    d_h,
    v_h,
    s_h,
    o_h,
    c_h,
    m_h,
    op_h,
    raw_ref,
    part_ref,
    ea_ref,
    eb_ref,
    buf,
    mbuf,
    opbuf,
    sums,
    prod,
    sems,
    op_sem,
):
    half = R // 2
    rows_all = tiles * R
    copies = []
    for i in range(2):
        rows = pl.ds(i * half, half)
        sources = [d_h.at[0], v_h.at[0], s_h.at[0, 0], s_h.at[1, 0], o_h.at[0], c_h.at[0]]
        group = [
            pltpu.make_async_copy(src.at[rows], buf.at[n, rows], sems.at[i, n])
            for n, src in enumerate(sources)
        ]
        group.append(pltpu.make_async_copy(m_h.at[0].at[rows], mbuf.at[rows], sems.at[i, 6]))
        copies.append(group)
    for copy in copies[0]:
        copy.start()
    for copy in copies[1]:
        copy.start()
    op_copy = pltpu.make_async_copy(op_h.at[0], opbuf, op_sem)
    op_copy.start()

    interval, cos, sin = scene_terms(scene, table)
    col = lax.broadcasted_iota(jnp.int32, (W, 128), 0) // 32
    lane = lax.broadcasted_iota(jnp.int32, (W, 128), 1) % 32
    gather_sum = jnp.where(col == lane, 1.0, 0.0).astype(BF16)
    zeros = jnp.zeros((PAD, W), F32)
    raw_ref[0:PAD, :] = zeros
    raw_ref[PAD + R : WIN, :] = zeros
    prod[0:PAD, :] = zeros[:, :128]
    prod[PAD + rows_all : PAD + rows_all + PAD, :] = zeros[:, :128]

    for i in range(2):
        for copy in copies[i]:
            copy.wait()
        rows = slice(i * half, (i + 1) * half)
        pred = (buf[0, rows] + interval * buf[1, rows]) + (cos * buf[2, rows] - sin * buf[3, rows])
        raw = buf[4, rows] - pred
        raw_ref[PAD + i * half : PAD + (i + 1) * half, :] = raw
        weighted = buf[5, rows] * mbuf[rows].astype(F32) * raw
        high = weighted.astype(BF16)
        low = (weighted - high.astype(F32)).astype(BF16)
        sums[rows] = jnp.dot(high, gather_sum, preferred_element_type=F32) + jnp.dot(
            low, gather_sum, preferred_element_type=F32
        )

    odd = lax.axis_index("tile") % 2 == 1
    first = raw_ref[PAD : PAD + 1, :]
    last = raw_ref[PAD + R - 1 : PAD + R, :]
    ea_ref[...] = jnp.where(odd, first, last)
    eb_ref[...] = jnp.where(odd, last, first)

    block_sums = (sums[...] * BLOCK_SCALE).astype(BF16)
    op_copy.wait()
    step = rows_all // 8
    for i in range(8):
        prod[PAD + i * step : PAD + (i + 1) * step, :] = jnp.dot(
            opbuf[i * step : (i + 1) * step, :], block_sums, preferred_element_type=F32
        )

    quarter = lax.broadcasted_iota(jnp.int32, (SUB, 128), 1) // 32

    def pack(k, carry):
        base = pl.multiple_of(k * R, 8)
        parts = [prod[pl.ds(base + SUB * g, SUB), :] for g in range(4)]
        low_half = jnp.where(quarter == 0, parts[0], parts[1])
        high_half = jnp.where(quarter == 2, parts[2], parts[3])
        part_ref[k] = jnp.where(quarter < 2, low_half, high_half).astype(BF16)
        return carry

    lax.fori_loop(0, tiles, pack, 0, unroll=8)


def front(tiles, scene, table, d, v, s, o, c, m, op):
    rows_all = tiles * R
    return pl.pallas_call(
        functools.partial(front_kernel, tiles),
        out_shape=(
            jax.ShapeDtypeStruct((WIN, W), F32),
            jax.ShapeDtypeStruct((tiles, SUB, 128), BF16),
            jax.ShapeDtypeStruct((1, W), F32),
            jax.ShapeDtypeStruct((1, W), F32),
        ),
        in_specs=[SMEM, SMEM] + [ANY] * 7,
        out_specs=(VMEM,) * 4,
        scratch_shapes=[
            pltpu.VMEM((6, R, W), F32),
            pltpu.VMEM((R, W), jnp.int32),
            pltpu.VMEM((rows_all, R), BF16),
            pltpu.VMEM((R, 128), F32),
            pltpu.VMEM((rows_all + 2 * PAD, 128), F32),
            pltpu.SemaphoreType.DMA((2, 7)),
            pltpu.SemaphoreType.DMA,
        ],
        cost_estimate=pl.CostEstimate(flops=10**8, bytes_accessed=4 * 10**6, transcendentals=0),
        name="front",
    )(scene, table, d, v, s, o, c, m, op)


def cov_kernel(
    scene, table, noise, d_ref, v_ref, s_ref, cd_ref, cc_ref, nv_ref, co_ref, va_ref, cov_ref, xg_ref, we_ref
):
    interval, cos, sin = scene_terms(scene, table)
    rows, cols = 8, 256
    across = W // cols

    def body(n, carry):
        r = pl.ds(pl.multiple_of((n // across) * rows, 8), rows)
        c = pl.ds(pl.multiple_of((n % across) * cols, 128), cols)
        x = [d_ref[0, r, c], v_ref[0, r, c], s_ref[0, 0, r, c], s_ref[1, 0, r, c]]
        diag = [cd_ref[i, 0, r, c] for i in range(4)]
        dev = [jnp.sqrt(e) for e in diag]
        p = [[None] * 4 for _ in range(4)]
        for i in range(4):
            p[i][i] = diag[i]
        for k, (i, j) in enumerate(PAIR_LIST):
            p[i][j] = p[j][i] = cc_ref[k, 0, r, c] * dev[i] * dev[j]
        q = [
            [p[0][j] + interval * p[1][j] for j in range(4)],
            [p[1][j] for j in range(4)],
            [cos * p[2][j] - sin * p[3][j] for j in range(4)],
            [sin * p[2][j] + cos * p[3][j] for j in range(4)],
        ]
        a = [[None] * 4 for _ in range(4)]
        for i in range(4):
            for j in range(i, 4):
                if j == 0:
                    e = q[i][0] + interval * q[i][1]
                elif j == 1:
                    e = q[i][1]
                elif j == 2:
                    e = cos * q[i][2] - sin * q[i][3]
                else:
                    e = sin * q[i][2] + cos * q[i][3]
                if i == j:
                    e = e + noise[i] * interval
                a[i][j] = a[j][i] = e
        pred = [
            x[0] + interval * x[1],
            x[1],
            cos * x[2] - sin * x[3],
            sin * x[2] + cos * x[3],
        ]
        coherence = co_ref[0, r, c]
        valid = va_ref[0, r, c].astype(F32)
        h = [a[i][0] + a[i][2] for i in range(4)]
        variance = h[0] + h[2] + nv_ref[0, r, c] / coherence
        scale = valid / variance
        gain = [h[i] * scale for i in range(4)]
        for i in range(4):
            xg_ref[i, r, c] = pred[i]
            xg_ref[4 + i, r, c] = gain[i]
            cov_ref[i, 0, r, c] = a[i][i] - gain[i] * h[i]
        for k, (i, j) in enumerate(PAIR_LIST):
            cov_ref[4 + k, 0, r, c] = a[i][j] - gain[i] * h[j]
        return carry

    lax.fori_loop(0, (d_ref.shape[1] // rows) * across, body, 0)
    weight = lambda c: co_ref[0, :, c : c + 128] * va_ref[0, :, c : c + 128].astype(F32)
    we_ref[:, :128] = weight(0)
    we_ref[:, 128:] = weight(W - 128)


def covariance(scene, table, noise, d, v, s, cd, cc, nv, co, va):
    step = 16
    plane = pl.BlockSpec((1, step, W), lambda i: (0, i, 0))
    planes = lambda n: pl.BlockSpec((n, 1, step, W), lambda i: (0, 0, i, 0))
    return pl.pallas_call(
        cov_kernel,
        grid=(R // step,),
        out_shape=(
            jax.ShapeDtypeStruct((10, 1, R, W), F32),
            jax.ShapeDtypeStruct((8, R, W), F32),
            jax.ShapeDtypeStruct((R, 256), F32),
        ),
        in_specs=[SMEM] * 3 + [plane, plane, planes(2), planes(4), planes(6), plane, plane, plane],
        out_specs=(
            planes(10),
            pl.BlockSpec((8, step, W), lambda i: (0, i, 0)),
            pl.BlockSpec((step, 256), lambda i: (i, 0)),
        ),
        cost_estimate=pl.CostEstimate(flops=2 * 10**7, bytes_accessed=12 * 10**6, transcendentals=0),
        name="covariance",
    )(scene, table, noise, d, v, s, cd, cc, nv, co, va)


def clean_window(cl, screen, raw_ref, pa_ref, pb_ref, blocks):
    odd = lax.axis_index("tile") % 2 == 1
    lane = lax.broadcasted_iota(jnp.int32, (SUB, 128), 1) // 32
    for g in range(4):
        rows = slice(g * SUB, (g + 1) * SUB)
        for n, b in enumerate(blocks):
            spread = jnp.take_along_axis(screen, lane + (32 * g + 4 * b), axis=1)
            cl[rows, 128 * n : 128 * (n + 1)] = raw_ref[rows, 128 * b : 128 * (b + 1)] - spread
    above = jnp.where(odd, pa_ref[...], pb_ref[...])
    below = jnp.where(odd, pb_ref[...], pa_ref[...])
    for n, b in enumerate(blocks):
        c = slice(128 * n, 128 * (n + 1))
        o = slice(128 * b, 128 * (b + 1))
        cl[PAD - 1 : PAD, c] = cl[PAD - 1 : PAD, c] + above[:, o]
        cl[PAD + R : PAD + R + 1, c] = cl[PAD + R : PAD + R + 1, c] + below[:, o]


def smoothed(up, mid, down):
    width = mid.shape[1]
    col = lax.broadcasted_iota(jnp.int32, mid.shape, 1)
    left = jnp.where(col == 0, 0.0, pltpu.roll(mid, 1, axis=1))
    right = jnp.where(col == width - 1, 0.0, pltpu.roll(mid, width - 1, axis=1))
    return (
        mid
        + ALONG_COEF * (up + down - 2.0 * mid)
        + ACROSS_COEF * (left + right - 2.0 * mid)
    )


def picks(index_row):
    rows = lax.broadcasted_iota(jnp.int32, (R, NB), 0)
    return jnp.where(rows == (index_row >> 3), 1.0, 0.0)


def margin_kernel(
    part_ref, raw_ref, pa_ref, pb_ref, we_ref, up_ref, down_ref, screen_ref, sm_ref, ma_ref, mb_ref, cl
):
    screen = jnp.sum(part_ref[...].astype(F32), axis=0)
    screen_ref[...] = screen
    clean_window(cl, screen, raw_ref, pa_ref, pb_ref, (0, 1, 6, 7))
    smooth = smoothed(cl[PAD - 1 : PAD - 1 + R], cl[PAD : PAD + R], cl[PAD + 1 : PAD + 1 + R])
    sm_ref[:, :128] = smooth[:, :128]
    sm_ref[:, 128:] = smooth[:, 384:]
    odd = lax.axis_index("track") % 2 == 1

    def payload(index_row, weight, value):
        pick = picks(index_row).astype(BF16)
        return [
            lax.dot_general(
                pick, e.astype(BF16), (((0,), (0,)), ((), ())), preferred_element_type=F32
            )
            for e in (weight * value, weight)
        ]

    going_down = payload(down_ref[0], we_ref[:, :128], smooth[:, :128])
    going_up = payload(up_ref[0], we_ref[:, 128:], smooth[:, 384:])
    for n in range(2):
        ma_ref[n] = jnp.where(odd, going_down[n], going_up[n]).astype(BF16)
        mb_ref[n] = jnp.where(odd, going_up[n], going_down[n]).astype(BF16)


def margin(part, raw, pa, pb, we, up, down):
    return pl.pallas_call(
        margin_kernel,
        out_shape=(
            jax.ShapeDtypeStruct((SUB, 128), F32),
            jax.ShapeDtypeStruct((R, 256), F32),
            jax.ShapeDtypeStruct((2, NB, 128), BF16),
            jax.ShapeDtypeStruct((2, NB, 128), BF16),
        ),
        in_specs=[VMEM] * 7,
        out_specs=(VMEM,) * 4,
        scratch_shapes=[pltpu.VMEM((WIN, 512), F32)],
        cost_estimate=pl.CostEstimate(flops=10**7, bytes_accessed=10**6, transcendentals=0),
        name="margin",
    )(part, raw, pa, pb, we, up, down)


def state_kernel(screen_ref, raw_ref, pa_ref, pb_ref, xg_ref, out_ref, cl):
    step = xg_ref.shape[1]

    @pl.when(pl.program_id(0) == 0)
    def _():
        clean_window(cl, screen_ref[...], raw_ref, pa_ref, pb_ref, tuple(range(8)))

    window = cl[pl.ds(pl.multiple_of(pl.program_id(0) * step, 8), step + 2 * PAD), :]
    smooth = smoothed(
        window[PAD - 1 : PAD - 1 + step], window[PAD : PAD + step], window[PAD + 1 : PAD + 1 + step]
    )
    for i in range(4):
        out_ref[i, 0] = xg_ref[i] + xg_ref[4 + i] * smooth


def state(screen, raw, pa, pb, xg):
    step = 16
    whole = lambda shape: pl.BlockSpec(shape, lambda i: (0,) * len(shape))
    return pl.pallas_call(
        state_kernel,
        grid=(R // step,),
        out_shape=jax.ShapeDtypeStruct((4, 1, R, W), F32),
        in_specs=[
            whole((SUB, 128)),
            whole((WIN, W)),
            whole((1, W)),
            whole((1, W)),
            pl.BlockSpec((8, step, W), lambda i: (0, i, 0)),
        ],
        out_specs=pl.BlockSpec((4, 1, step, W), lambda i: (0, 0, i, 0)),
        scratch_shapes=[pltpu.VMEM((WIN, W), F32)],
        cost_estimate=pl.CostEstimate(flops=2 * 10**6, bytes_accessed=4 * 10**6, transcendentals=0),
        name="state",
    )(screen, raw, pa, pb, xg)


def finish_kernel(ra_ref, rb_ref, up_ref, down_ref, sm_ref, we_ref, xg_ref, _, out_ref):
    side = pl.program_id(0)
    odd = lax.axis_index("track") % 2
    use_a = odd != side
    index_row = jnp.where(side == 1, up_ref[0], down_ref[0])
    place = picks(index_row).astype(BF16)
    got = [
        jnp.dot(place, jnp.where(use_a, ra_ref[n].astype(F32), rb_ref[n].astype(F32)).astype(BF16), preferred_element_type=F32)
        for n in range(2)
    ]
    weight = we_ref[...] + WEIGHT_FLOOR
    innovation = (weight * sm_ref[...] + got[0]) / (weight + got[1])
    for i in range(4):
        out_ref[i, 0] = xg_ref[i] + xg_ref[4 + i] * innovation


def finish(ra, rb, up, down, sm, we, xg, ns):
    whole = lambda shape: pl.BlockSpec(shape, lambda i: (0,) * len(shape))
    edge = pl.BlockSpec((R, 128), lambda i: (0, i))
    return pl.pallas_call(
        finish_kernel,
        grid=(2,),
        out_shape=jax.ShapeDtypeStruct(ns.shape, F32),
        in_specs=[
            whole((2, NB, 128)),
            whole((2, NB, 128)),
            whole((1, 1, NB)),
            whole((1, 1, NB)),
            edge,
            edge,
            pl.BlockSpec((8, R, 128), lambda i: (0, 0, 7 * i)),
            ANY,
        ],
        out_specs=pl.BlockSpec((4, 1, R, 128), lambda i: (0, 0, 0, 7 * i)),
        input_output_aliases={7: 0},
        cost_estimate=pl.CostEstimate(flops=10**6, bytes_accessed=10**6, transcendentals=0),
        name="finish",
    )(ra, rb, up, down, sm, we, xg, ns)


def swap(value, axis, first):
    count = lax.axis_size(axis)
    pairs = []
    for i in range(first, count - 1, 2):
        pairs += [(i, i + 1), (i + 1, i)]
    return lax.ppermute(value, axis, pairs)


def local(
    displacement,
    velocity,
    seasonal,
    cov_diag,
    cov_corr,
    observed,
    noise_var,
    coherence,
    valid,
    screen_operator,
    process_noise,
    track_scene,
    scene_interval,
    margin_up,
    margin_down,
):
    tiles = lax.axis_size("tile")
    raw, part, edge_a, edge_b = front(
        tiles, track_scene, scene_interval, displacement, velocity, seasonal, observed, coherence, valid, screen_operator
    )
    part = lax.all_to_all(part, "tile", split_axis=0, concat_axis=0, tiled=True)
    near_a = swap(edge_a, "tile", 0)
    near_b = swap(edge_b, "tile", 1)
    new_cov, xg, edge_weight = covariance(
        track_scene,
        scene_interval,
        process_noise,
        displacement,
        velocity,
        seasonal,
        cov_diag,
        cov_corr,
        noise_var,
        coherence,
        valid,
    )
    screen, edge_smooth, out_a, out_b = margin(
        part, raw, near_a, near_b, edge_weight, margin_up, margin_down
    )
    in_a = swap(out_a, "track", 0)
    in_b = swap(out_b, "track", 1)
    new_state = state(screen, raw, near_a, near_b, xg)
    new_state = finish(in_a, in_b, margin_up, margin_down, edge_smooth, edge_weight, xg, new_state)
    return new_state, new_cov


def solution(mesh):
    in_specs = (
        P("track", "tile", None),
        P("track", "tile", None),
        P(None, "track", "tile", None),
        P(None, "track", "tile", None),
        P(None, "track", "tile", None),
        P("track", "tile", None),
        P("track", "tile", None),
        P("track", "tile", None),
        P("track", "tile", None),
        P("track", None, "tile"),
        P(),
        P("track"),
        P(),
        P("track", "tile", None),
        P("track", "tile", None),
    )
    out_specs = (P(None, "track", "tile", None), P(None, "track", "tile", None))
    return jax.shard_map(local, mesh=mesh, in_specs=in_specs, out_specs=out_specs, check_vma=False)
```

time: 114 us -> 53 us (0.46)
  the two profiles are of different devices: /device:TPU:27 before, /device:TPU:1 now
where the time goes in v1:
time: 53 us; the launch traced here: 52.5 us
  starting transfers between devices  22.5 us (42%)
  Pallas kernels  21.6 us (41%)
  local copies, waits for them, and re-layouts  3.69 us (7%)
  waiting for transfers between devices  3.33 us (6%)
  between operations  1.37 us (3%)
    all_to_all x1, starting transfers between devices, local(): part = lax.all_to_all(part, 'tile', split_axis=0, concat_axis=0, tiled=True)  13.6 us
    ppermute x4, starting transfers between devices, swap(): return lax.ppermute(value, axis, pairs)  8.94 us
    pallas_call x1, Pallas kernels, covariance(): pl.pallas_call(cov_kernel, grid=(R // step,), out_shape=(jax.ShapeDtypeSt...  7.8 us
    pallas_call x1, Pallas kernels, state(): pl.pallas_call(state_kernel, grid=(R // step,), out_shape=jax.ShapeDtypeS...  5.02 us
    pallas_call x1, Pallas kernels, front(): pl.pallas_call(functools.partial(front_kernel, tiles), out_shape=(jax.Sha...  4.47 us
    unnamed x11, local copies, waits for them, and re-layouts  3.69 us
    all_to_all x1, waiting for transfers between devices, local(): part = lax.all_to_all(part, 'tile', split_axis=0, concat_axis=0, tiled=True)  3.32 us
    pallas_call x1, Pallas kernels, margin(): pl.pallas_call(margin_kernel, out_shape=(jax.ShapeDtypeStruct((SUB, 128),...  2.23 us
  transfers between devices with their start and end apart: 5, of which 1 were waited for; matrix products, arithmetic and copies ran while one was open for 0% of the time, Pallas kernels for 24%

profile of v1, /device:TPU:1, one launch (start us, length us, event | category | flops | bytes accessed | tf_op | source)
XLA Modules:
  0.0 52.5 jit_solution(14060793352888041993)
XLA Ops:
  1.3 2.3 %copy.18.op_h = bf16[1,5120,80]{2,1,0:T(8,128)(2,1)} copy(bf16[1,5120,80]{1,2,0:T(8,128)(2,1)} %param.24) | data formatting | bytes 1638400 | tf_op args[9]
  3.6 4.5 %front.1 = (f32[96,1024]{1,0:T(8,128)}, bf16[64,24,128]{2,1,0:T(8,128)(2,1)}, f32[1,1024]{1,0:T(1,128)}, f32[1,1024]{1,0:T(1,128)}) custom-call(s32[1]{0:T(128)S(6)} %copy.20.scene, f32[16]{0:T(128)} %table.3, f32[1,80,1024]{2,1,0:T(8,128)} %d_ref.1, f32[1,80,1024]{2,1,0:T(8,128)} %v_ref.1, f32[2,1,80,1024]{3,2,1,0:T(8,128)} %s_ref.1, f32[1,80,1024]{2,1,0:T(8,128)} %o_h.1, ...), custom_call_target="tpu_custom_call" | custom-call | flops 100000000 | bytes 4000000 | tf_op jit(solution)/shard_map/front/pallas_call | solution.py:133
  8.1 13.6 %all-to-all-start = ((bf16[64,24,128]{2,1,0:T(8,128)(2,1)}), bf16[64,24,128]{2,1,0:T(8,128)(2,1)S(1)}, u32[]{:S(2)}, u32[]{:S(2)}) async-start(bf16[64,24,128]{2,1,0:T(8,128)(2,1)} %get-tuple-element.13), calls=%async_computation | async-start | bytes 786432 | tf_op jit(solution)/shard_map/all_to_all | solution.py:427
  21.7 1.1 %collective-permute-start = (f32[1,1024]{1,0:T(1,128)}, f32[1,1024]{1,0:T(1,128)S(1)}, u32[]{:S(2)}, u32[]{:S(2)}) collective-permute-start(f32[1,1024]{1,0:T(1,128)} %get-tuple-element.15), channel_id=1, source_target_pairs={{0,1},{1,0},{2,3},{3,2},{4,5},{5,4},{6,7},{7,6},{8,9},{9,8},{10,11... | collective-permute-start | bytes 12296 | tf_op jit(solution)/shard_map/ppermute | solution.py:403
  22.8 0.6 %collective-permute-start.1 = (f32[1,1024]{1,0:T(1,128)}, f32[1,1024]{1,0:T(1,128)S(1)}, u32[]{:S(2)}, u32[]{:S(2)}) collective-permute-start(f32[1,1024]{1,0:T(1,128)} %get-tuple-element.16), channel_id=1, source_target_pairs={{1,2},{2,1},{3,4},{4,3},{5,6},{6,5},{7,8},{8,7},{9,10},{10,9},{11,... | collective-permute-start | bytes 12296 | tf_op jit(solution)/shard_map/ppermute | solution.py:403
  23.4 7.8 %covariance.1 = (f32[10,1,80,1024]{3,2,1,0:T(8,128)}, f32[8,80,1024]{2,1,0:T(8,128)}, f32[80,256]{1,0:T(8,128)}) custom-call(s32[1]{0:T(128)S(6)} %copy.20.scene, f32[16]{0:T(128)} %table.3, f32[4]{0:T(128)} %noise.1, f32[1,80,1024]{2,1,0:T(8,128)} %d_ref.1, f32[1,80,1024]{2,1,0:T(8,128)} %v_ref.1, f32[2,1,80,1024]{3,2,1,0:T(8,128)} %s_ref.1, ...), custom_call_target="tpu_custom_call" | custom-call | flops 20000000 | bytes 12000000 | tf_op jit(solution)/shard_map/covariance/pallas_call | solution.py:225
  31.3 0.0 collective-permute-done.pa_ref
  31.3 0.0 copy-start.3
  31.3 0.0 collective-permute-done.1.pb_ref
  31.3 0.0 copy-start.4
  31.3 3.3 %all-to-all-done.part_ref = bf16[64,24,128]{2,1,0:T(8,128)(2,1)S(1)} async-done(((bf16[64,24,128]{2,1,0:T(8,128)(2,1)}), bf16[64,24,128]{2,1,0:T(8,128)(2,1)S(1)}, u32[]{:S(2)}, u32[]{:S(2)}) %all-to-all-start) | async-done | bytes 393248 | tf_op jit(solution)/shard_map/all_to_all | solution.py:427
  34.6 0.0 copy-start
  34.6 0.0 copy-done.3
  34.6 0.0 copy-done.4
  34.6 0.7 %copy-done = bf16[64,24,128]{2,1,0:T(8,128)(2,1)} copy-done((bf16[64,24,128]{2,1,0:T(8,128)(2,1)}, bf16[64,24,128]{2,1,0:T(8,128)(2,1)S(1)}, u32[]{:S(2)}) %copy-start) | copy-done | bytes 393240
  35.4 2.2 %margin.1 = (f32[24,128]{1,0:T(8,128)}, f32[80,256]{1,0:T(8,128)}, bf16[2,40,128]{2,1,0:T(8,128)(2,1)}, bf16[2,40,128]{2,1,0:T(8,128)(2,1)}) custom-call(bf16[64,24,128]{2,1,0:T(8,128)(2,1)} %copy-done, f32[96,1024]{1,0:T(8,128)} %get-tuple-element.14.raw_ref, f32[1,1024]{1,0:T(1,128)} %copy-done.3, f32[1,1024]{1,0:T(1,128)} %copy-done.4, ...), custom_call_target="tpu_custom_call" | custom-call | flops 10000000 | bytes 1000000 | tf_op jit(solution)/shard_map/margin/pallas_call | solution.py:306
  37.6 3.0 %collective-permute-start.2 = (bf16[2,40,128]{2,1,0:T(8,128)(2,1)}, bf16[2,40,128]{2,1,0:T(8,128)(2,1)S(1)}, u32[]{:S(2)}, u32[]{:S(2)}) collective-permute-start(bf16[2,40,128]{2,1,0:T(8,128)(2,1)} %get-tuple-element.18), channel_id=1, source_target_pairs={{0,64},{64,0},{128,192},{192,128},{1,65},{65,1},{129,193},{193,129... | collective-permute-start | bytes 61448 | tf_op jit(solution)/shard_map/ppermute | solution.py:403
  40.6 4.2 %collective-permute-start.3 = (bf16[2,40,128]{2,1,0:T(8,128)(2,1)}, bf16[2,40,128]{2,1,0:T(8,128)(2,1)S(1)}, u32[]{:S(2)}, u32[]{:S(2)}) collective-permute-start(bf16[2,40,128]{2,1,0:T(8,128)(2,1)} %get-tuple-element.19), channel_id=1, source_target_pairs={{64,128},{128,64},{65,129},{129,65},{66,130},{130,66},{67,131},{13... | collective-permute-start | bytes 61448 | tf_op jit(solution)/shard_map/ppermute | solution.py:403
  44.8 5.0 %state.1._ = f32[4,1,80,1024]{3,2,1,0:T(8,128)} custom-call(f32[24,128]{1,0:T(8,128)} %get-tuple-element.22.screen_ref, f32[96,1024]{1,0:T(8,128)} %get-tuple-element.14.raw_ref, f32[1,1024]{1,0:T(1,128)} %copy-done.3, f32[1,1024]{1,0:T(1,128)} %copy-done.4, f32[8,80,1024]{2,1,0:T(8,128)} %get-tuple-element.21.xg_ref), custom_call_target="tpu_custom_call" | custom-call | flops 2000000 | bytes 4000000 | tf_op jit(solution)/shard_map/state/pallas_call | solution.py:340
  49.8 0.0 collective-permute-done.2.ra_ref
  49.8 0.0 copy-start.1
  49.8 0.0 collective-permute-done.3.rb_ref
  49.8 0.0 copy-start.2
  49.8 0.6 %copy-done.1 = bf16[2,40,128]{2,1,0:T(8,128)(2,1)} copy-done((bf16[2,40,128]{2,1,0:T(8,128)(2,1)}, bf16[2,40,128]{2,1,0:T(8,128)(2,1)S(1)}, u32[]{:S(2)}) %copy-start.1) | copy-done | bytes 20504
  50.4 0.0 copy-done.2
  50.4 2.1 %finish.1 = f32[4,1,80,1024]{3,2,1,0:T(8,128)} custom-call(bf16[2,40,128]{2,1,0:T(8,128)(2,1)} %copy-done.1, bf16[2,40,128]{2,1,0:T(8,128)(2,1)} %copy-done.2, s32[1,1,40]{2,1,0:T(1,128)} %up_ref.3, s32[1,1,40]{2,1,0:T(1,128)} %down_ref.3, f32[80,256]{1,0:T(8,128)} %get-tuple-element.20.sm_ref, ...), custom_call_target="tpu_custom_call", output_to_operand_aliasing={{}: (7, {})} | custom-call | flops 1000000 | bytes 1000000 | tf_op jit(solution)/shard_map/finish/pallas_call | solution.py:377
Async XLA Ops:
  8.1 26.5 %all-to-all-start = ((bf16[64,24,128]{2,1,0:T(8,128)(2,1)}), bf16[64,24,128]{2,1,0:T(8,128)(2,1)S(1)}, u32[]{:S(2)}, u32[]{:S(2)}) async-start(bf16[64,24,128]{2,1,0:T(8,128)(2,1)} %get-tuple-element.13), calls=%async_computation | async-start | bytes 786432 | tf_op jit(solution)/shard_map/all_to_all | solution.py:427
  21.7 9.6 %collective-permute-start = (f32[1,1024]{1,0:T(1,128)}, f32[1,1024]{1,0:T(1,128)S(1)}, u32[]{:S(2)}, u32[]{:S(2)}) collective-permute-start(f32[1,1024]{1,0:T(1,128)} %get-tuple-element.15), channel_id=1, source_target_pairs={{0,1},{1,0},{2,3},{3,2},{4,5},{5,4},{6,7},{7,6},{8,9},{9,8},{10,11... | collective-permute-start | bytes 12296 | tf_op jit(solution)/shard_map/ppermute | solution.py:403
  22.8 8.5 %collective-permute-start.1 = (f32[1,1024]{1,0:T(1,128)}, f32[1,1024]{1,0:T(1,128)S(1)}, u32[]{:S(2)}, u32[]{:S(2)}) collective-permute-start(f32[1,1024]{1,0:T(1,128)} %get-tuple-element.16), channel_id=1, source_target_pairs={{1,2},{2,1},{3,4},{4,3},{5,6},{6,5},{7,8},{8,7},{9,10},{10,9},{11,... | collective-permute-start | bytes 12296 | tf_op jit(solution)/shard_map/ppermute | solution.py:403
  31.3 3.4 %copy-start.3 = (f32[1,1024]{1,0:T(1,128)}, f32[1,1024]{1,0:T(1,128)S(1)}, u32[]{:S(2)}) copy-start(f32[1,1024]{1,0:T(1,128)S(1)} %collective-permute-done.pa_ref) | copy-start | bytes 12292
  31.3 3.3 %copy-start.4 = (f32[1,1024]{1,0:T(1,128)}, f32[1,1024]{1,0:T(1,128)S(1)}, u32[]{:S(2)}) copy-start(f32[1,1024]{1,0:T(1,128)S(1)} %collective-permute-done.1.pb_ref) | copy-start | bytes 12292
  34.6 0.7 %copy-start = (bf16[64,24,128]{2,1,0:T(8,128)(2,1)}, bf16[64,24,128]{2,1,0:T(8,128)(2,1)S(1)}, u32[]{:S(2)}) copy-start(bf16[64,24,128]{2,1,0:T(8,128)(2,1)S(1)} %all-to-all-done.part_ref) | copy-start | bytes 1179652
  37.6 12.2 %collective-permute-start.2 = (bf16[2,40,128]{2,1,0:T(8,128)(2,1)}, bf16[2,40,128]{2,1,0:T(8,128)(2,1)S(1)}, u32[]{:S(2)}, u32[]{:S(2)}) collective-permute-start(bf16[2,40,128]{2,1,0:T(8,128)(2,1)} %get-tuple-element.18), channel_id=1, source_target_pairs={{0,64},{64,0},{128,192},{192,128},{1,65},{65,1},{129,193},{193,129... | collective-permute-start | bytes 61448 | tf_op jit(solution)/shard_map/ppermute | solution.py:403
  40.6 9.3 %collective-permute-start.3 = (bf16[2,40,128]{2,1,0:T(8,128)(2,1)}, bf16[2,40,128]{2,1,0:T(8,128)(2,1)S(1)}, u32[]{:S(2)}, u32[]{:S(2)}) collective-permute-start(bf16[2,40,128]{2,1,0:T(8,128)(2,1)} %get-tuple-element.19), channel_id=1, source_target_pairs={{64,128},{128,64},{65,129},{129,65},{66,130},{130,66},{67,131},{13... | collective-permute-start | bytes 61448 | tf_op jit(solution)/shard_map/ppermute | solution.py:403
  49.8 0.6 %copy-start.1 = (bf16[2,40,128]{2,1,0:T(8,128)(2,1)}, bf16[2,40,128]{2,1,0:T(8,128)(2,1)S(1)}, u32[]{:S(2)}) copy-start(bf16[2,40,128]{2,1,0:T(8,128)(2,1)S(1)} %collective-permute-done.2.ra_ref) | copy-start | bytes 61444
  49.8 0.6 %copy-start.2 = (bf16[2,40,128]{2,1,0:T(8,128)(2,1)}, bf16[2,40,128]{2,1,0:T(8,128)(2,1)S(1)}, u32[]{:S(2)}) copy-start(bf16[2,40,128]{2,1,0:T(8,128)(2,1)S(1)} %collective-permute-done.3.rb_ref) | copy-start | bytes 61444

commit v2 on v1

--- a/solution.py
+++ b/solution.py
@@ -29,6 +29,14 @@
 ANY = pl.BlockSpec(memory_space=pl.ANY)
 
 
+def hbm(x):
+    return pltpu.with_memory_space_constraint(x, pltpu.HBM)
+
+
+def vmem(x):
+    return pltpu.with_memory_space_constraint(x, pltpu.VMEM)
+
+
 def scene_terms(scene, table):
     interval = table[scene[0]]
     angle = jnp.full((1, 1), SEASON_RATE * interval, F32)
@@ -37,8 +45,8 @@
 
 def front_kernel(
     tiles,
-    scene,
-    table,
+    scene_h,
+    table_h,
     d_h,
     v_h,
     s_h,
@@ -50,14 +58,24 @@
     part_ref,
     ea_ref,
     eb_ref,
+    terms_ref,
     buf,
     mbuf,
     opbuf,
     sums,
     prod,
+    scene,
+    table,
     sems,
     op_sem,
+    scalar_sems,
 ):
+    scalar_copies = [
+        pltpu.make_async_copy(scene_h, scene, scalar_sems.at[0]),
+        pltpu.make_async_copy(table_h, table, scalar_sems.at[1]),
+    ]
+    for copy in scalar_copies:
+        copy.start()
     half = R // 2
     rows_all = tiles * R
     copies = []
@@ -77,7 +95,6 @@
     op_copy = pltpu.make_async_copy(op_h.at[0], opbuf, op_sem)
     op_copy.start()
 
-    interval, cos, sin = scene_terms(scene, table)
     col = lax.broadcasted_iota(jnp.int32, (W, 128), 0) // 32
     lane = lax.broadcasted_iota(jnp.int32, (W, 128), 1) % 32
     gather_sum = jnp.where(col == lane, 1.0, 0.0).astype(BF16)
@@ -87,6 +104,11 @@
     prod[0:PAD, :] = zeros[:, :128]
     prod[PAD + rows_all : PAD + rows_all + PAD, :] = zeros[:, :128]
 
+    for copy in scalar_copies:
+        copy.wait()
+    interval, cos, sin = scene_terms(scene, table)
+    for n, term in enumerate((interval, cos, sin)):
+        terms_ref[n : n + 1, :] = jnp.broadcast_to(term, (1, 128))
     for i in range(2):
         for copy in copies[i]:
             copy.wait()
@@ -111,8 +133,11 @@
     op_copy.wait()
     step = rows_all // 8
     for i in range(8):
-        prod[PAD + i * step : PAD + (i + 1) * step, :] = jnp.dot(
-            opbuf[i * step : (i + 1) * step, :], block_sums, preferred_element_type=F32
+        prod[PAD + i * step : PAD + (i + 1) * step, :] = lax.dot_general(
+            opbuf[:, i * step : (i + 1) * step],
+            block_sums,
+            (((0,), (0,)), ((), ())),
+            preferred_element_type=F32,
         )
 
     quarter = lax.broadcasted_iota(jnp.int32, (SUB, 128), 1) // 32
@@ -133,31 +158,36 @@
     return pl.pallas_call(
         functools.partial(front_kernel, tiles),
         out_shape=(
-            jax.ShapeDtypeStruct((WIN, W), F32),
+            pltpu.VMEM((WIN, W), F32),
             jax.ShapeDtypeStruct((tiles, SUB, 128), BF16),
             jax.ShapeDtypeStruct((1, W), F32),
             jax.ShapeDtypeStruct((1, W), F32),
+            pltpu.VMEM((8, 128), F32),
         ),
-        in_specs=[SMEM, SMEM] + [ANY] * 7,
-        out_specs=(VMEM,) * 4,
+        in_specs=[ANY] * 9,
+        out_specs=(VMEM,) * 5,
         scratch_shapes=[
             pltpu.VMEM((6, R, W), F32),
             pltpu.VMEM((R, W), jnp.int32),
-            pltpu.VMEM((rows_all, R), BF16),
+            pltpu.VMEM((R, rows_all), BF16),
             pltpu.VMEM((R, 128), F32),
             pltpu.VMEM((rows_all + 2 * PAD, 128), F32),
+            pltpu.SMEM((1,), jnp.int32),
+            pltpu.SMEM((16,), F32),
             pltpu.SemaphoreType.DMA((2, 7)),
             pltpu.SemaphoreType.DMA,
+            pltpu.SemaphoreType.DMA((2,)),
         ],
         cost_estimate=pl.CostEstimate(flops=10**8, bytes_accessed=4 * 10**6, transcendentals=0),
+        compiler_params=pltpu.CompilerParams(vmem_limit_bytes=12 * 2**20),
         name="front",
-    )(scene, table, d, v, s, o, c, m, op)
+    )(scene, *map(hbm, (table, d, v, s, o, c, m, op)))
 
 
 def cov_kernel(
-    scene, table, noise, d_ref, v_ref, s_ref, cd_ref, cc_ref, nv_ref, co_ref, va_ref, cov_ref, xg_ref, we_ref
+    terms, noise, d_ref, v_ref, s_ref, cd_ref, cc_ref, nv_ref, co_ref, va_ref, cov_ref, xg_ref, we_ref
 ):
-    interval, cos, sin = scene_terms(scene, table)
+    interval, cos, sin = [terms[n : n + 1, 0:1] for n in range(3)]
     rows, cols = 8, 256
     across = W // cols
 
@@ -218,7 +248,7 @@
     we_ref[:, 128:] = weight(W - 128)
 
 
-def covariance(scene, table, noise, d, v, s, cd, cc, nv, co, va):
+def covariance(terms, noise, d, v, s, cd, cc, nv, co, va):
     step = 16
     plane = pl.BlockSpec((1, step, W), lambda i: (0, i, 0))
     planes = lambda n: pl.BlockSpec((n, 1, step, W), lambda i: (0, 0, i, 0))
@@ -227,18 +257,19 @@
         grid=(R // step,),
         out_shape=(
             jax.ShapeDtypeStruct((10, 1, R, W), F32),
-            jax.ShapeDtypeStruct((8, R, W), F32),
-            jax.ShapeDtypeStruct((R, 256), F32),
+            pltpu.VMEM((8, R, W), F32),
+            pltpu.VMEM((R, 256), F32),
         ),
-        in_specs=[SMEM] * 3 + [plane, plane, planes(2), planes(4), planes(6), plane, plane, plane],
+        in_specs=[pl.BlockSpec((8, 128), lambda i: (0, 0)), SMEM] + [plane, plane, planes(2), planes(4), planes(6), plane, plane, plane],
         out_specs=(
             planes(10),
             pl.BlockSpec((8, step, W), lambda i: (0, i, 0)),
             pl.BlockSpec((step, 256), lambda i: (i, 0)),
         ),
         cost_estimate=pl.CostEstimate(flops=2 * 10**7, bytes_accessed=12 * 10**6, transcendentals=0),
+        compiler_params=pltpu.CompilerParams(vmem_limit_bytes=8 * 2**20),
         name="covariance",
-    )(scene, table, noise, d, v, s, cd, cc, nv, co, va)
+    )(vmem(terms), noise, *map(hbm, (d, v, s, cd, cc, nv, co, va)))
 
 
 def clean_window(cl, screen, raw_ref, pa_ref, pb_ref, blocks):
@@ -306,8 +337,8 @@
     return pl.pallas_call(
         margin_kernel,
         out_shape=(
-            jax.ShapeDtypeStruct((SUB, 128), F32),
-            jax.ShapeDtypeStruct((R, 256), F32),
+            pltpu.VMEM((SUB, 128), F32),
+            pltpu.VMEM((R, 256), F32),
             jax.ShapeDtypeStruct((2, NB, 128), BF16),
             jax.ShapeDtypeStruct((2, NB, 128), BF16),
         ),
@@ -315,8 +346,9 @@
         out_specs=(VMEM,) * 4,
         scratch_shapes=[pltpu.VMEM((WIN, 512), F32)],
         cost_estimate=pl.CostEstimate(flops=10**7, bytes_accessed=10**6, transcendentals=0),
+        compiler_params=pltpu.CompilerParams(vmem_limit_bytes=2 * 2**20),
         name="margin",
-    )(part, raw, pa, pb, we, up, down)
+    )(part, vmem(raw), pa, pb, vmem(we), up, down)
 
 
 def state_kernel(screen_ref, raw_ref, pa_ref, pb_ref, xg_ref, out_ref, cl):
@@ -340,7 +372,7 @@
     return pl.pallas_call(
         state_kernel,
         grid=(R // step,),
-        out_shape=jax.ShapeDtypeStruct((4, 1, R, W), F32),
+        out_shape=pltpu.HBM((4, 1, R, W), F32),
         in_specs=[
             whole((SUB, 128)),
             whole((WIN, W)),
@@ -351,8 +383,9 @@
         out_specs=pl.BlockSpec((4, 1, step, W), lambda i: (0, 0, i, 0)),
         scratch_shapes=[pltpu.VMEM((WIN, W), F32)],
         cost_estimate=pl.CostEstimate(flops=2 * 10**6, bytes_accessed=4 * 10**6, transcendentals=0),
+        compiler_params=pltpu.CompilerParams(vmem_limit_bytes=6 * 2**20),
         name="state",
-    )(screen, raw, pa, pb, xg)
+    )(vmem(screen), vmem(raw), pa, pb, vmem(xg))
 
 
 def finish_kernel(ra_ref, rb_ref, up_ref, down_ref, sm_ref, we_ref, xg_ref, _, out_ref):
@@ -391,8 +424,9 @@
         out_specs=pl.BlockSpec((4, 1, R, 128), lambda i: (0, 0, 0, 7 * i)),
         input_output_aliases={7: 0},
         cost_estimate=pl.CostEstimate(flops=10**6, bytes_accessed=10**6, transcendentals=0),
+        compiler_params=pltpu.CompilerParams(vmem_limit_bytes=3 * 2**20),
         name="finish",
-    )(ra, rb, up, down, sm, we, xg, ns)
+    )(ra, rb, up, down, vmem(sm), vmem(we), vmem(xg), ns)
 
 
 def swap(value, axis, first):
@@ -421,15 +455,14 @@
     margin_down,
 ):
     tiles = lax.axis_size("tile")
-    raw, part, edge_a, edge_b = front(
-        tiles, track_scene, scene_interval, displacement, velocity, seasonal, observed, coherence, valid, screen_operator
+    raw, part, edge_a, edge_b, terms = front(
+        tiles, track_scene, scene_interval, displacement, velocity, seasonal, observed, coherence, valid, jnp.swapaxes(screen_operator, 1, 2)
     )
     part = lax.all_to_all(part, "tile", split_axis=0, concat_axis=0, tiled=True)
     near_a = swap(edge_a, "tile", 0)
     near_b = swap(edge_b, "tile", 1)
     new_cov, xg, edge_weight = covariance(
-        track_scene,
-        scene_interval,
+        terms,
         process_noise,
         displacement,
         velocity,

time: 53 us -> 43.7 us (0.82)
  Pallas kernels: 21.6 us -> 14.8 us
  local copies, waits for them, and re-layouts: 3.69 us -> 0.02 us
  waiting for transfers between devices: 3.33 us -> 4.48 us
    pallas_call x3, Pallas kernels: 11.7 us -> 6.97 us  [the longest x1 3.59 us: front(): pl.pallas_call(functools.partial(front_kernel, tiles), out_shape=(pltpu.V...]
    unnamed x11 -> x6, local copies, waits for them, and re-layouts: 3.69 us -> 0.02 us
    pallas_call x1, Pallas kernels: 7.8 us -> 6.65 us  [covariance(): pl.pallas_call(cov_kernel, grid=(R // step,), out_shape=(jax.ShapeDtypeSt...]
    all_to_all x1, waiting for transfers between devices: 3.32 us -> 4.46 us  [local(): part = lax.all_to_all(part, 'tile', split_axis=0, concat_axis=0, tiled=True)]
    pallas_call x1, Pallas kernels: 2.09 us -> 1.2 us  [finish(): pl.pallas_call(finish_kernel, grid=(2,), out_shape=jax.ShapeDtypeStruct(n...]
  transfers between devices with their start and end apart: 5 -> 5, of which waited for: 1 -> 1; matrix products, arithmetic and copies ran while one was open for 0% -> 0% of each run, Pallas kernels for 24% -> 22%
where the time goes in v2:
time: 43.7 us; the launch traced here: 43.3 us
  starting transfers between devices  22.6 us (52%)
  Pallas kernels  14.8 us (34%)
  waiting for transfers between devices  4.48 us (10%)
  between operations  1.38 us (3%)
    all_to_all x1, starting transfers between devices, local(): part = lax.all_to_all(part, 'tile', split_axis=0, concat_axis=0, tiled=True)  13.6 us
    ppermute x4, starting transfers between devices, swap(): return lax.ppermute(value, axis, pairs)  9.05 us
    pallas_call x1, Pallas kernels, covariance(): pl.pallas_call(cov_kernel, grid=(R // step,), out_shape=(jax.ShapeDtypeSt...  6.65 us
    all_to_all x1, waiting for transfers between devices, local(): part = lax.all_to_all(part, 'tile', split_axis=0, concat_axis=0, tiled=True)  4.46 us
    pallas_call x1, Pallas kernels, front(): pl.pallas_call(functools.partial(front_kernel, tiles), out_shape=(pltpu.V...  3.59 us
    pallas_call x1, Pallas kernels, state(): pl.pallas_call(state_kernel, grid=(R // step,), out_shape=pltpu.HBM((4, 1...  2.92 us
    pallas_call x1, Pallas kernels, finish(): pl.pallas_call(finish_kernel, grid=(2,), out_shape=jax.ShapeDtypeStruct(n...  1.2 us
  transfers between devices with their start and end apart: 5, of which 1 were waited for; matrix products, arithmetic and copies ran while one was open for 0% of the time, Pallas kernels for 22%

profile of v2, /device:TPU:1, one launch (start us, length us, event | category | flops | bytes accessed | tf_op | source)
XLA Modules:
  0.0 43.3 jit_solution(10767031589162676131)
XLA Ops:
  0.6 0.0 copy-start.2
  1.3 3.6 %front.1 = (f32[96,1024]{1,0:T(8,128)S(1)}, bf16[64,24,128]{2,1,0:T(8,128)(2,1)}, f32[1,1024]{1,0:T(1,128)S(1)}, f32[1,1024]{1,0:T(1,128)S(1)}, f32[8,128]{1,0:T(8,128)S(1)}) custom-call(s32[1]{0:T(128)S(6)} %copy.19.scene_h, f32[16]{0:T(128)} %table_h.1, f32[1,80,1024]{2,1,0:T(8,128)} %d_ref.1, f32[1,80,1024]{2,1,0:T(8,128)} %v_ref.1, ...), custom_call_target="tpu_custom_call" | custom-call | flops 100000000 | bytes 4000000 | tf_op jit(solution)/shard_map/front/pallas_call | solution.py:158
  4.9 13.6 %all-to-all-start = ((bf16[64,24,128]{2,1,0:T(8,128)(2,1)}), bf16[64,24,128]{2,1,0:T(8,128)(2,1)S(1)}, u32[]{:S(2)}, u32[]{:S(2)}) async-start(bf16[64,24,128]{2,1,0:T(8,128)(2,1)} %get-tuple-element.14), calls=%async_computation | async-start | bytes 786432 | tf_op jit(solution)/shard_map/all_to_all | solution.py:461
  18.5 1.1 %collective-permute-start = (f32[1,1024]{1,0:T(1,128)S(1)}, f32[1,1024]{1,0:T(1,128)S(1)}, u32[]{:S(2)}, u32[]{:S(2)}) collective-permute-start(f32[1,1024]{1,0:T(1,128)S(1)} %get-tuple-element.16), channel_id=1, source_target_pairs={{0,1},{1,0},{2,3},{3,2},{4,5},{5,4},{6,7},{7,6},{8,9},{9,8},{10,11... | collective-permute-start | bytes 12296 | tf_op jit(solution)/shard_map/ppermute | solution.py:437
  19.6 0.6 %collective-permute-start.1 = (f32[1,1024]{1,0:T(1,128)S(1)}, f32[1,1024]{1,0:T(1,128)S(1)}, u32[]{:S(2)}, u32[]{:S(2)}) collective-permute-start(f32[1,1024]{1,0:T(1,128)S(1)} %get-tuple-element.17), channel_id=1, source_target_pairs={{1,2},{2,1},{3,4},{4,3},{5,6},{6,5},{7,8},{8,7},{9,10},{10,9},{11,... | collective-permute-start | bytes 12296 | tf_op jit(solution)/shard_map/ppermute | solution.py:437
  20.2 0.0 copy-done.2
  20.2 0.0 copy-start
  20.3 0.0 copy-start.1
  20.3 6.7 %covariance.1 = (f32[10,1,80,1024]{3,2,1,0:T(8,128)}, f32[8,80,1024]{2,1,0:T(8,128)S(1)}, f32[80,256]{1,0:T(8,128)S(1)}) custom-call(f32[8,128]{1,0:T(8,128)S(1)} %get-tuple-element.18.terms, f32[4]{0:T(128)S(1)} %copy-done.2, f32[1,80,1024]{2,1,0:T(8,128)} %d_ref.1, f32[1,80,1024]{2,1,0:T(8,128)} %v_ref.1, f32[2,1,80,1024]{3,2,1,0:T(8,128)} %s_ref.1, ...), custom_call_target="tpu_custom_call" | custom-call | flops 20000000 | bytes 12000000 | tf_op jit(solution)/shard_map/covariance/pallas_call | solution.py:255
  26.9 0.0 collective-permute-done.pa_ref
  26.9 0.0 collective-permute-done.1.pb_ref
  26.9 4.5 %all-to-all-done.part_ref = bf16[64,24,128]{2,1,0:T(8,128)(2,1)S(1)} async-done(((bf16[64,24,128]{2,1,0:T(8,128)(2,1)}), bf16[64,24,128]{2,1,0:T(8,128)(2,1)S(1)}, u32[]{:S(2)}, u32[]{:S(2)}) %all-to-all-start) | async-done | bytes 393248 | tf_op jit(solution)/shard_map/all_to_all | solution.py:461
  31.4 0.0 copy-done
  31.4 0.0 copy-done.1
  31.4 0.5 %margin.1 = (f32[24,128]{1,0:T(8,128)S(1)}, f32[80,256]{1,0:T(8,128)S(1)}, bf16[2,40,128]{2,1,0:T(8,128)(2,1)S(1)}, bf16[2,40,128]{2,1,0:T(8,128)(2,1)S(1)}) custom-call(bf16[64,24,128]{2,1,0:T(8,128)(2,1)S(1)} %all-to-all-done.part_ref, f32[96,1024]{1,0:T(8,128)S(1)} %get-tuple-element.15.raw_ref, f32[1,1024]{1,0:T(1,128)S(1)} %collective-permute-done.pa_ref, ...), custom_call_target="tpu_custom_call" | custom-call | flops 10000000 | bytes 1000000 | tf_op jit(solution)/shard_map/margin/pallas_call | solution.py:337
  31.9 3.1 %collective-permute-start.2 = (bf16[2,40,128]{2,1,0:T(8,128)(2,1)S(1)}, bf16[2,40,128]{2,1,0:T(8,128)(2,1)S(1)}, u32[]{:S(2)}, u32[]{:S(2)}) collective-permute-start(bf16[2,40,128]{2,1,0:T(8,128)(2,1)S(1)} %get-tuple-element.20), channel_id=1, source_target_pairs={{0,64},{64,0},{128,192},{192,128},{1,65},{65,1},{129,193},{193,129... | collective-permute-start | bytes 61448 | tf_op jit(solution)/shard_map/ppermute | solution.py:437
  34.9 4.3 %collective-permute-start.3 = (bf16[2,40,128]{2,1,0:T(8,128)(2,1)S(1)}, bf16[2,40,128]{2,1,0:T(8,128)(2,1)S(1)}, u32[]{:S(2)}, u32[]{:S(2)}) collective-permute-start(bf16[2,40,128]{2,1,0:T(8,128)(2,1)S(1)} %get-tuple-element.21), channel_id=1, source_target_pairs={{64,128},{128,64},{65,129},{129,65},{66,130},{130,66},{67,131},{13... | collective-permute-start | bytes 61448 | tf_op jit(solution)/shard_map/ppermute | solution.py:437
  39.2 2.9 %state.1._ = f32[4,1,80,1024]{3,2,1,0:T(8,128)} custom-call(f32[24,128]{1,0:T(8,128)S(1)} %get-tuple-element.24.screen_ref, f32[96,1024]{1,0:T(8,128)S(1)} %get-tuple-element.15.raw_ref, f32[1,1024]{1,0:T(1,128)S(1)} %collective-permute-done.pa_ref, f32[1,1024]{1,0:T(1,128)S(1)} %collective-permute-done.1.pb_ref, f32[8,80,1024]{2,1,0:T(8,128)S(1)} %get-tuple-element.23.xg_ref), custom_call_target="tpu_custom_call" | custom-call | flops 2000000 | bytes 4000000 | tf_op jit(solution)/shard_map/state/pallas_call | solution.py:372
  42.1 0.0 collective-permute-done.2.ra_ref
  42.1 0.0 collective-permute-done.3.rb_ref
  42.1 1.2 %finish.1 = f32[4,1,80,1024]{3,2,1,0:T(8,128)} custom-call(bf16[2,40,128]{2,1,0:T(8,128)(2,1)S(1)} %collective-permute-done.2.ra_ref, bf16[2,40,128]{2,1,0:T(8,128)(2,1)S(1)} %collective-permute-done.3.rb_ref, s32[1,1,40]{2,1,0:T(1,128)S(1)} %copy-done, s32[1,1,40]{2,1,0:T(1,128)S(1)} %copy-done.1, ...), custom_call_target="tpu_custom_call", output_to_operand_aliasing={{}: (7, {})} | custom-call | flops 1000000 | bytes 1000000 | tf_op jit(solution)/shard_map/finish/pallas_call | solution.py:410
Async XLA Ops:
  0.6 19.6 %copy-start.2 = (f32[4]{0:T(128)S(1)}, f32[4]{0:T(128)}, u32[]{:S(2)}) copy-start(f32[4]{0:T(128)} %noise.1) | copy-start | bytes 52
  4.9 26.5 %all-to-all-start = ((bf16[64,24,128]{2,1,0:T(8,128)(2,1)}), bf16[64,24,128]{2,1,0:T(8,128)(2,1)S(1)}, u32[]{:S(2)}, u32[]{:S(2)}) async-start(bf16[64,24,128]{2,1,0:T(8,128)(2,1)} %get-tuple-element.14), calls=%async_computation | async-start | bytes 786432 | tf_op jit(solution)/shard_map/all_to_all | solution.py:461
  18.5 8.4 %collective-permute-start = (f32[1,1024]{1,0:T(1,128)S(1)}, f32[1,1024]{1,0:T(1,128)S(1)}, u32[]{:S(2)}, u32[]{:S(2)}) collective-permute-start(f32[1,1024]{1,0:T(1,128)S(1)} %get-tuple-element.16), channel_id=1, source_target_pairs={{0,1},{1,0},{2,3},{3,2},{4,5},{5,4},{6,7},{7,6},{8,9},{9,8},{10,11... | collective-permute-start | bytes 12296 | tf_op jit(solution)/shard_map/ppermute | solution.py:437
  19.6 7.4 %collective-permute-start.1 = (f32[1,1024]{1,0:T(1,128)S(1)}, f32[1,1024]{1,0:T(1,128)S(1)}, u32[]{:S(2)}, u32[]{:S(2)}) collective-permute-start(f32[1,1024]{1,0:T(1,128)S(1)} %get-tuple-element.17), channel_id=1, source_target_pairs={{1,2},{2,1},{3,4},{4,3},{5,6},{6,5},{7,8},{8,7},{9,10},{10,9},{11,... | collective-permute-start | bytes 12296 | tf_op jit(solution)/shard_map/ppermute | solution.py:437
  20.2 11.2 %copy-start = (s32[1,1,40]{2,1,0:T(1,128)S(1)}, s32[1,1,40]{2,1,0:T(1,128)}, u32[]{:S(2)}) copy-start(s32[1,1,40]{2,1,0:T(1,128)} %up_ref.3) | copy-start | bytes 484
  20.3 11.2 %copy-start.1 = (s32[1,1,40]{2,1,0:T(1,128)S(1)}, s32[1,1,40]{2,1,0:T(1,128)}, u32[]{:S(2)}) copy-start(s32[1,1,40]{2,1,0:T(1,128)} %down_ref.3) | copy-start | bytes 484
  31.9 10.2 %collective-permute-start.2 = (bf16[2,40,128]{2,1,0:T(8,128)(2,1)S(1)}, bf16[2,40,128]{2,1,0:T(8,128)(2,1)S(1)}, u32[]{:S(2)}, u32[]{:S(2)}) collective-permute-start(bf16[2,40,128]{2,1,0:T(8,128)(2,1)S(1)} %get-tuple-element.20), channel_id=1, source_target_pairs={{0,64},{64,0},{128,192},{192,128},{1,65},{65,1},{129,193},{193,129... | collective-permute-start | bytes 61448 | tf_op jit(solution)/shard_map/ppermute | solution.py:437
  34.9 7.2 %collective-permute-start.3 = (bf16[2,40,128]{2,1,0:T(8,128)(2,1)S(1)}, bf16[2,40,128]{2,1,0:T(8,128)(2,1)S(1)}, u32[]{:S(2)}, u32[]{:S(2)}) collective-permute-start(bf16[2,40,128]{2,1,0:T(8,128)(2,1)S(1)} %get-tuple-element.21), channel_id=1, source_target_pairs={{64,128},{128,64},{65,129},{129,65},{66,130},{130,66},{67,131},{13... | collective-permute-start | bytes 61448 | tf_op jit(solution)/shard_map/ppermute | solution.py:437

commit v3 on v2

--- a/solution.py
+++ b/solution.py
@@ -123,11 +123,13 @@
             low, gather_sum, preferred_element_type=F32
         )
 
-    odd = lax.axis_index("tile") % 2 == 1
+    tile = lax.axis_index("tile")
+    odd = tile % 2 == 1
     first = raw_ref[PAD : PAD + 1, :]
     last = raw_ref[PAD + R - 1 : PAD + R, :]
     ea_ref[...] = jnp.where(odd, first, last)
-    eb_ref[...] = jnp.where(odd, last, first)
+    at_end = (tile == 0) | (tile == tiles - 1)
+    eb_ref[...] = jnp.where(at_end, 0.0, jnp.where(odd, last, first))
 
     block_sums = (sums[...] * BLOCK_SCALE).astype(BF16)
     op_copy.wait()
@@ -432,8 +434,9 @@
 def swap(value, axis, first):
     count = lax.axis_size(axis)
     pairs = []
-    for i in range(first, count - 1, 2):
-        pairs += [(i, i + 1), (i + 1, i)]
+    for i in range(first, first + count, 2):
+        a, b = i % count, (i + 1) % count
+        pairs += [(a, b), (b, a)]
     return lax.ppermute(value, axis, pairs)
 
 
@@ -476,8 +479,8 @@
     screen, edge_smooth, out_a, out_b = margin(
         part, raw, near_a, near_b, edge_weight, margin_up, margin_down
     )
+    in_b = swap(out_b, "track", 1)
     in_a = swap(out_a, "track", 0)
-    in_b = swap(out_b, "track", 1)
     new_state = state(screen, raw, near_a, near_b, xg)
     new_state = finish(in_a, in_b, margin_up, margin_down, edge_smooth, edge_weight, xg, new_state)
     return new_state, new_cov

time: 43.7 us -> 41.8 us (0.957)
  waiting for transfers between devices: 4.48 us -> 0.36 us
  starting transfers between devices: 22.6 us -> 25 us
    all_to_all x1, waiting for transfers between devices: 4.46 us -> 0.35 us  [local(): part = lax.all_to_all(part, 'tile', split_axis=0, concat_axis=0, tiled=True)]
    ppermute x4, starting transfers between devices: 9.05 us -> 11.4 us  [swap(): return lax.ppermute(value, axis, pairs)]
  transfers between devices with their start and end apart: 5 -> 5, of which waited for: 1 -> 1; matrix products, arithmetic and copies ran while one was open for 0% -> 0% of each run, Pallas kernels for 22% -> 23%
where the time goes in v3:
time: 41.8 us; the launch traced here: 41.5 us
  starting transfers between devices  25 us (60%)
  Pallas kernels  14.8 us (35%)
  between operations  1.34 us (3%)
    all_to_all x1, starting transfers between devices, local(): part = lax.all_to_all(part, 'tile', split_axis=0, concat_axis=0, tiled=True)  13.6 us
    ppermute x4, starting transfers between devices, swap(): return lax.ppermute(value, axis, pairs)  11.4 us
    pallas_call x1, Pallas kernels, covariance(): pl.pallas_call(cov_kernel, grid=(R // step,), out_shape=(jax.ShapeDtypeSt...  6.65 us
    pallas_call x1, Pallas kernels, front(): pl.pallas_call(functools.partial(front_kernel, tiles), out_shape=(pltpu.V...  3.59 us
    pallas_call x1, Pallas kernels, state(): pl.pallas_call(state_kernel, grid=(R // step,), out_shape=pltpu.HBM((4, 1...  2.91 us
    pallas_call x1, Pallas kernels, finish(): pl.pallas_call(finish_kernel, grid=(2,), out_shape=jax.ShapeDtypeStruct(n...  1.19 us
  transfers between devices with their start and end apart: 5, of which 1 were waited for; matrix products, arithmetic and copies ran while one was open for 0% of the time, Pallas kernels for 23%

profile of v3, /device:TPU:1, one launch (start us, length us, event | category | flops | bytes accessed | tf_op | source)
XLA Modules:
  0.0 41.5 jit_solution(16710242151725150895)
XLA Ops:
  0.6 0.0 copy-start.2
  1.3 3.6 %front.1 = (f32[96,1024]{1,0:T(8,128)S(1)}, bf16[64,24,128]{2,1,0:T(8,128)(2,1)}, f32[1,1024]{1,0:T(1,128)S(1)}, f32[1,1024]{1,0:T(1,128)S(1)}, f32[8,128]{1,0:T(8,128)S(1)}) custom-call(s32[1]{0:T(128)S(6)} %copy.19.scene_h, f32[16]{0:T(128)} %table_h.1, f32[1,80,1024]{2,1,0:T(8,128)} %d_ref.1, f32[1,80,1024]{2,1,0:T(8,128)} %v_ref.1, ...), custom_call_target="tpu_custom_call" | custom-call | flops 100000000 | bytes 4000000 | tf_op jit(solution)/shard_map/front/pallas_call | solution.py:160
  4.9 13.6 %all-to-all-start = ((bf16[64,24,128]{2,1,0:T(8,128)(2,1)}), bf16[64,24,128]{2,1,0:T(8,128)(2,1)S(1)}, u32[]{:S(2)}, u32[]{:S(2)}) async-start(bf16[64,24,128]{2,1,0:T(8,128)(2,1)} %get-tuple-element.14), calls=%async_computation | async-start | bytes 786432 | tf_op jit(solution)/shard_map/all_to_all | solution.py:464
  18.5 1.1 %collective-permute-start = (f32[1,1024]{1,0:T(1,128)S(1)}, f32[1,1024]{1,0:T(1,128)S(1)}, u32[]{:S(2)}, u32[]{:S(2)}) collective-permute-start(f32[1,1024]{1,0:T(1,128)S(1)} %get-tuple-element.16), channel_id=1, source_target_pairs={{0,1},{1,0},{2,3},{3,2},{4,5},{5,4},{6,7},{7,6},{8,9},{9,8},{10,11... | collective-permute-start | bytes 12296 | tf_op jit(solution)/shard_map/ppermute | solution.py:440
  19.6 4.8 %collective-permute-start.1 = (f32[1,1024]{1,0:T(1,128)S(1)}, f32[1,1024]{1,0:T(1,128)S(1)}, u32[]{:S(2)}, u32[]{:S(2)}) collective-permute-start(f32[1,1024]{1,0:T(1,128)S(1)} %get-tuple-element.17), channel_id=1, source_target_pairs={{1,2},{2,1},{3,4},{4,3},{5,6},{6,5},{7,8},{8,7},{9,10},{10,9},{11,... | collective-permute-start | bytes 12296 | tf_op jit(solution)/shard_map/ppermute | solution.py:440
  24.4 0.0 copy-done.2
  24.4 0.0 copy-start
  24.4 0.0 copy-start.1
  24.4 6.6 %covariance.1 = (f32[10,1,80,1024]{3,2,1,0:T(8,128)}, f32[8,80,1024]{2,1,0:T(8,128)S(1)}, f32[80,256]{1,0:T(8,128)S(1)}) custom-call(f32[8,128]{1,0:T(8,128)S(1)} %get-tuple-element.18.terms, f32[4]{0:T(128)S(1)} %copy-done.2, f32[1,80,1024]{2,1,0:T(8,128)} %d_ref.1, f32[1,80,1024]{2,1,0:T(8,128)} %v_ref.1, f32[2,1,80,1024]{3,2,1,0:T(8,128)} %s_ref.1, ...), custom_call_target="tpu_custom_call" | custom-call | flops 20000000 | bytes 12000000 | tf_op jit(solution)/shard_map/covariance/pallas_call | solution.py:257
  31.0 0.0 collective-permute-done.pa_ref
  31.1 0.0 collective-permute-done.1.pb_ref
  31.1 0.3 all-to-all-done.part_ref
  31.4 0.0 copy-done
  31.4 0.0 copy-done.1
  31.4 0.5 %margin.1 = (f32[24,128]{1,0:T(8,128)S(1)}, f32[80,256]{1,0:T(8,128)S(1)}, bf16[2,40,128]{2,1,0:T(8,128)(2,1)S(1)}, bf16[2,40,128]{2,1,0:T(8,128)(2,1)S(1)}) custom-call(bf16[64,24,128]{2,1,0:T(8,128)(2,1)S(1)} %all-to-all-done.part_ref, f32[96,1024]{1,0:T(8,128)S(1)} %get-tuple-element.15.raw_ref, f32[1,1024]{1,0:T(1,128)S(1)} %collective-permute-done.pa_ref, ...), custom_call_target="tpu_custom_call" | custom-call | flops 10000000 | bytes 1000000 | tf_op jit(solution)/shard_map/margin/pallas_call | solution.py:339
  31.9 3.1 %collective-permute-start.2 = (bf16[2,40,128]{2,1,0:T(8,128)(2,1)S(1)}, bf16[2,40,128]{2,1,0:T(8,128)(2,1)S(1)}, u32[]{:S(2)}, u32[]{:S(2)}) collective-permute-start(bf16[2,40,128]{2,1,0:T(8,128)(2,1)S(1)} %get-tuple-element.20), channel_id=1, source_target_pairs={{0,64},{64,0},{128,192},{192,128},{1,65},{65,1},{129,193},{193,129... | collective-permute-start | bytes 61448 | tf_op jit(solution)/shard_map/ppermute | solution.py:440
  34.9 2.4 %collective-permute-start.3 = (bf16[2,40,128]{2,1,0:T(8,128)(2,1)S(1)}, bf16[2,40,128]{2,1,0:T(8,128)(2,1)S(1)}, u32[]{:S(2)}, u32[]{:S(2)}) collective-permute-start(bf16[2,40,128]{2,1,0:T(8,128)(2,1)S(1)} %get-tuple-element.21), channel_id=1, source_target_pairs={{64,128},{128,64},{192,0},{0,192},{65,129},{129,65},{193,1},{1,193... | collective-permute-start | bytes 61448 | tf_op jit(solution)/shard_map/ppermute | solution.py:440
  37.4 2.9 %state.1._ = f32[4,1,80,1024]{3,2,1,0:T(8,128)} custom-call(f32[24,128]{1,0:T(8,128)S(1)} %get-tuple-element.24.screen_ref, f32[96,1024]{1,0:T(8,128)S(1)} %get-tuple-element.15.raw_ref, f32[1,1024]{1,0:T(1,128)S(1)} %collective-permute-done.pa_ref, f32[1,1024]{1,0:T(1,128)S(1)} %collective-permute-done.1.pb_ref, f32[8,80,1024]{2,1,0:T(8,128)S(1)} %get-tuple-element.23.xg_ref), custom_call_target="tpu_custom_call" | custom-call | flops 2000000 | bytes 4000000 | tf_op jit(solution)/shard_map/state/pallas_call | solution.py:374
  40.3 0.0 collective-permute-done.2.ra_ref
  40.3 0.0 collective-permute-done.3.rb_ref
  40.3 1.2 %finish.1 = f32[4,1,80,1024]{3,2,1,0:T(8,128)} custom-call(bf16[2,40,128]{2,1,0:T(8,128)(2,1)S(1)} %collective-permute-done.2.ra_ref, bf16[2,40,128]{2,1,0:T(8,128)(2,1)S(1)} %collective-permute-done.3.rb_ref, s32[1,1,40]{2,1,0:T(1,128)S(1)} %copy-done, s32[1,1,40]{2,1,0:T(1,128)S(1)} %copy-done.1, ...), custom_call_target="tpu_custom_call", output_to_operand_aliasing={{}: (7, {})} | custom-call | flops 1000000 | bytes 1000000 | tf_op jit(solution)/shard_map/finish/pallas_call | solution.py:412
Async XLA Ops:
  0.6 23.8 %copy-start.2 = (f32[4]{0:T(128)S(1)}, f32[4]{0:T(128)}, u32[]{:S(2)}) copy-start(f32[4]{0:T(128)} %noise.1) | copy-start | bytes 52
  4.9 26.5 %all-to-all-start = ((bf16[64,24,128]{2,1,0:T(8,128)(2,1)}), bf16[64,24,128]{2,1,0:T(8,128)(2,1)S(1)}, u32[]{:S(2)}, u32[]{:S(2)}) async-start(bf16[64,24,128]{2,1,0:T(8,128)(2,1)} %get-tuple-element.14), calls=%async_computation | async-start | bytes 786432 | tf_op jit(solution)/shard_map/all_to_all | solution.py:464
  18.5 12.6 %collective-permute-start = (f32[1,1024]{1,0:T(1,128)S(1)}, f32[1,1024]{1,0:T(1,128)S(1)}, u32[]{:S(2)}, u32[]{:S(2)}) collective-permute-start(f32[1,1024]{1,0:T(1,128)S(1)} %get-tuple-element.16), channel_id=1, source_target_pairs={{0,1},{1,0},{2,3},{3,2},{4,5},{5,4},{6,7},{7,6},{8,9},{9,8},{10,11... | collective-permute-start | bytes 12296 | tf_op jit(solution)/shard_map/ppermute | solution.py:440
  19.6 11.5 %collective-permute-start.1 = (f32[1,1024]{1,0:T(1,128)S(1)}, f32[1,1024]{1,0:T(1,128)S(1)}, u32[]{:S(2)}, u32[]{:S(2)}) collective-permute-start(f32[1,1024]{1,0:T(1,128)S(1)} %get-tuple-element.17), channel_id=1, source_target_pairs={{1,2},{2,1},{3,4},{4,3},{5,6},{6,5},{7,8},{8,7},{9,10},{10,9},{11,... | collective-permute-start | bytes 12296 | tf_op jit(solution)/shard_map/ppermute | solution.py:440
  24.4 7.0 %copy-start = (s32[1,1,40]{2,1,0:T(1,128)S(1)}, s32[1,1,40]{2,1,0:T(1,128)}, u32[]{:S(2)}) copy-start(s32[1,1,40]{2,1,0:T(1,128)} %up_ref.3) | copy-start | bytes 484
  24.4 7.0 %copy-start.1 = (s32[1,1,40]{2,1,0:T(1,128)S(1)}, s32[1,1,40]{2,1,0:T(1,128)}, u32[]{:S(2)}) copy-start(s32[1,1,40]{2,1,0:T(1,128)} %down_ref.3) | copy-start | bytes 484
  31.9 8.4 %collective-permute-start.2 = (bf16[2,40,128]{2,1,0:T(8,128)(2,1)S(1)}, bf16[2,40,128]{2,1,0:T(8,128)(2,1)S(1)}, u32[]{:S(2)}, u32[]{:S(2)}) collective-permute-start(bf16[2,40,128]{2,1,0:T(8,128)(2,1)S(1)} %get-tuple-element.20), channel_id=1, source_target_pairs={{0,64},{64,0},{128,192},{192,128},{1,65},{65,1},{129,193},{193,129... | collective-permute-start | bytes 61448 | tf_op jit(solution)/shard_map/ppermute | solution.py:440
  34.9 5.4 %collective-permute-start.3 = (bf16[2,40,128]{2,1,0:T(8,128)(2,1)S(1)}, bf16[2,40,128]{2,1,0:T(8,128)(2,1)S(1)}, u32[]{:S(2)}, u32[]{:S(2)}) collective-permute-start(bf16[2,40,128]{2,1,0:T(8,128)(2,1)S(1)} %get-tuple-element.21), channel_id=1, source_target_pairs={{64,128},{128,64},{192,0},{0,192},{65,129},{129,65},{193,1},{1,193... | collective-permute-start | bytes 61448 | tf_op jit(solution)/shard_map/ppermute | solution.py:440

commit v4 on v3

--- a/solution.py
+++ b/solution.py
@@ -8,6 +8,7 @@
 from jax.experimental.pallas import tpu as pltpu
 from jax.sharding import PartitionSpec as P
 
+
 SEASON_RATE = 2.0 * math.pi * 12.0 / 365.25
 ALONG_COEF = 0.2
 ACROSS_COEF = 0.1
@@ -21,6 +22,7 @@
 WIN = R + 2 * PAD
 SUB = WIN // 4
 NB = 40
+SHARE = 16
 F32 = jnp.float32
 BF16 = jnp.bfloat16
 
@@ -62,13 +64,15 @@
     buf,
     mbuf,
     opbuf,
-    sums,
+    split,
     prod,
+    packed,
     scene,
     table,
     sems,
     op_sem,
     scalar_sems,
+    out_sems,
 ):
     scalar_copies = [
         pltpu.make_async_copy(scene_h, scene, scalar_sems.at[0]),
@@ -76,11 +80,11 @@
     ]
     for copy in scalar_copies:
         copy.start()
-    half = R // 2
+    cuts = ((0, 48), (48, 32))
     rows_all = tiles * R
     copies = []
     for i in range(2):
-        rows = pl.ds(i * half, half)
+        rows = pl.ds(*cuts[i])
         sources = [d_h.at[0], v_h.at[0], s_h.at[0, 0], s_h.at[1, 0], o_h.at[0], c_h.at[0]]
         group = [
             pltpu.make_async_copy(src.at[rows], buf.at[n, rows], sems.at[i, n])
@@ -112,16 +116,19 @@
     for i in range(2):
         for copy in copies[i]:
             copy.wait()
-        rows = slice(i * half, (i + 1) * half)
-        pred = (buf[0, rows] + interval * buf[1, rows]) + (cos * buf[2, rows] - sin * buf[3, rows])
-        raw = buf[4, rows] - pred
-        raw_ref[PAD + i * half : PAD + (i + 1) * half, :] = raw
-        weighted = buf[5, rows] * mbuf[rows].astype(F32) * raw
-        high = weighted.astype(BF16)
-        low = (weighted - high.astype(F32)).astype(BF16)
-        sums[rows] = jnp.dot(high, gather_sum, preferred_element_type=F32) + jnp.dot(
-            low, gather_sum, preferred_element_type=F32
-        )
+        at, size = cuts[i]
+        for r0 in range(at, at + size, 16):
+            for c0 in range(0, W, 256):
+                r, c = slice(r0, r0 + 16), slice(c0, c0 + 256)
+                pred = (buf[0, r, c] + interval * buf[1, r, c]) + (
+                    cos * buf[2, r, c] - sin * buf[3, r, c]
+                )
+                raw = buf[4, r, c] - pred
+                raw_ref[PAD + r0 : PAD + r0 + 16, c] = raw
+                weighted = buf[5, r, c] * mbuf[r, c].astype(F32) * raw
+                high = weighted.astype(BF16)
+                split[r, c] = high
+                split[R + r0 : R + r0 + 16, c] = (weighted - high.astype(F32)).astype(BF16)
 
     tile = lax.axis_index("tile")
     odd = tile % 2 == 1
@@ -131,7 +138,8 @@
     at_end = (tile == 0) | (tile == tiles - 1)
     eb_ref[...] = jnp.where(at_end, 0.0, jnp.where(odd, last, first))
 
-    block_sums = (sums[...] * BLOCK_SCALE).astype(BF16)
+    sums = jnp.dot(split[...], gather_sum, preferred_element_type=F32)
+    block_sums = ((sums[:R] + sums[R:]) * BLOCK_SCALE).astype(BF16)
     op_copy.wait()
     step = rows_all // 8
     for i in range(8):
@@ -149,10 +157,17 @@
         parts = [prod[pl.ds(base + SUB * g, SUB), :] for g in range(4)]
         low_half = jnp.where(quarter == 0, parts[0], parts[1])
         high_half = jnp.where(quarter == 2, parts[2], parts[3])
-        part_ref[k] = jnp.where(quarter < 2, low_half, high_half).astype(BF16)
+        packed[k] = jnp.where(quarter < 2, low_half, high_half).astype(BF16)
         return carry
 
-    lax.fori_loop(0, tiles, pack, 0, unroll=8)
+    sent = []
+    for n in range(tiles // SHARE):
+        lax.fori_loop(n * SHARE, (n + 1) * SHARE, pack, 0, unroll=8)
+        span = pl.ds(n * SHARE, SHARE)
+        sent.append(pltpu.make_async_copy(packed.at[span], part_ref.at[span], out_sems.at[n]))
+        sent[-1].start()
+    for copy in sent:
+        copy.wait()
 
 
 def front(tiles, scene, table, d, v, s, o, c, m, op):
@@ -161,24 +176,26 @@
         functools.partial(front_kernel, tiles),
         out_shape=(
             pltpu.VMEM((WIN, W), F32),
-            jax.ShapeDtypeStruct((tiles, SUB, 128), BF16),
+            pltpu.HBM((tiles, SUB, 128), BF16),
             jax.ShapeDtypeStruct((1, W), F32),
             jax.ShapeDtypeStruct((1, W), F32),
             pltpu.VMEM((8, 128), F32),
         ),
         in_specs=[ANY] * 9,
-        out_specs=(VMEM,) * 5,
+        out_specs=(VMEM, ANY, VMEM, VMEM, VMEM),
         scratch_shapes=[
             pltpu.VMEM((6, R, W), F32),
             pltpu.VMEM((R, W), jnp.int32),
             pltpu.VMEM((R, rows_all), BF16),
-            pltpu.VMEM((R, 128), F32),
+            pltpu.VMEM((2 * R, W), BF16),
             pltpu.VMEM((rows_all + 2 * PAD, 128), F32),
+            pltpu.VMEM((tiles, SUB, 128), BF16),
             pltpu.SMEM((1,), jnp.int32),
             pltpu.SMEM((16,), F32),
             pltpu.SemaphoreType.DMA((2, 7)),
             pltpu.SemaphoreType.DMA,
             pltpu.SemaphoreType.DMA((2,)),
+            pltpu.SemaphoreType.DMA((tiles // SHARE,)),
         ],
         cost_estimate=pl.CostEstimate(flops=10**8, bytes_accessed=4 * 10**6, transcendentals=0),
         compiler_params=pltpu.CompilerParams(vmem_limit_bytes=12 * 2**20),
@@ -251,7 +268,7 @@
 
 
 def covariance(terms, noise, d, v, s, cd, cc, nv, co, va):
-    step = 16
+    step = 40
     plane = pl.BlockSpec((1, step, W), lambda i: (0, i, 0))
     planes = lambda n: pl.BlockSpec((n, 1, step, W), lambda i: (0, 0, i, 0))
     return pl.pallas_call(
@@ -269,7 +286,7 @@
             pl.BlockSpec((step, 256), lambda i: (i, 0)),
         ),
         cost_estimate=pl.CostEstimate(flops=2 * 10**7, bytes_accessed=12 * 10**6, transcendentals=0),
-        compiler_params=pltpu.CompilerParams(vmem_limit_bytes=8 * 2**20),
+        compiler_params=pltpu.CompilerParams(vmem_limit_bytes=24 * 2**20),
         name="covariance",
     )(vmem(terms), noise, *map(hbm, (d, v, s, cd, cc, nv, co, va)))
 
@@ -353,77 +370,79 @@
     )(part, vmem(raw), pa, pb, vmem(we), up, down)
 
 
-def state_kernel(screen_ref, raw_ref, pa_ref, pb_ref, xg_ref, out_ref, cl):
-    step = xg_ref.shape[1]
-
-    @pl.when(pl.program_id(0) == 0)
-    def _():
-        clean_window(cl, screen_ref[...], raw_ref, pa_ref, pb_ref, tuple(range(8)))
-
-    window = cl[pl.ds(pl.multiple_of(pl.program_id(0) * step, 8), step + 2 * PAD), :]
-    smooth = smoothed(
-        window[PAD - 1 : PAD - 1 + step], window[PAD : PAD + step], window[PAD + 1 : PAD + 1 + step]
-    )
-    for i in range(4):
-        out_ref[i, 0] = xg_ref[i] + xg_ref[4 + i] * smooth
+def state_kernel(screen_ref, raw_ref, pa_ref, pb_ref, xg_ref, out_ref, cl, held, sems):
+    clean_window(cl, screen_ref[...], raw_ref, pa_ref, pb_ref, tuple(range(8)))
+    step = R // 5
+    copies = []
+    for n in range(5):
+        r0 = n * step
+        rows = slice(r0, r0 + step)
+        smooth = smoothed(
+            cl[PAD - 1 + r0 : PAD - 1 + r0 + step],
+            cl[PAD + r0 : PAD + r0 + step],
+            cl[PAD + 1 + r0 : PAD + 1 + r0 + step],
+        )
+        for i in range(4):
+            held[i, rows] = xg_ref[i, rows] + xg_ref[4 + i, rows] * smooth
+        span = pl.ds(r0, step)
+        copies.append(
+            pltpu.make_async_copy(held.at[:, span], out_ref.at[:, 0, span], sems.at[n])
+        )
+        copies[-1].start()
+    for copy in copies:
+        copy.wait()
 
 
 def state(screen, raw, pa, pb, xg):
-    step = 16
-    whole = lambda shape: pl.BlockSpec(shape, lambda i: (0,) * len(shape))
     return pl.pallas_call(
         state_kernel,
-        grid=(R // step,),
         out_shape=pltpu.HBM((4, 1, R, W), F32),
-        in_specs=[
-            whole((SUB, 128)),
-            whole((WIN, W)),
-            whole((1, W)),
-            whole((1, W)),
-            pl.BlockSpec((8, step, W), lambda i: (0, i, 0)),
+        in_specs=[VMEM] * 5,
+        out_specs=ANY,
+        scratch_shapes=[
+            pltpu.VMEM((WIN, W), F32),
+            pltpu.VMEM((4, R, W), F32),
+            pltpu.SemaphoreType.DMA((5,)),
         ],
-        out_specs=pl.BlockSpec((4, 1, step, W), lambda i: (0, 0, i, 0)),
-        scratch_shapes=[pltpu.VMEM((WIN, W), F32)],
         cost_estimate=pl.CostEstimate(flops=2 * 10**6, bytes_accessed=4 * 10**6, transcendentals=0),
         compiler_params=pltpu.CompilerParams(vmem_limit_bytes=6 * 2**20),
         name="state",
     )(vmem(screen), vmem(raw), pa, pb, vmem(xg))
 
 
-def finish_kernel(ra_ref, rb_ref, up_ref, down_ref, sm_ref, we_ref, xg_ref, _, out_ref):
-    side = pl.program_id(0)
-    odd = lax.axis_index("track") % 2
-    use_a = odd != side
-    index_row = jnp.where(side == 1, up_ref[0], down_ref[0])
-    place = picks(index_row).astype(BF16)
-    got = [
-        jnp.dot(place, jnp.where(use_a, ra_ref[n].astype(F32), rb_ref[n].astype(F32)).astype(BF16), preferred_element_type=F32)
-        for n in range(2)
-    ]
-    weight = we_ref[...] + WEIGHT_FLOOR
-    innovation = (weight * sm_ref[...] + got[0]) / (weight + got[1])
-    for i in range(4):
-        out_ref[i, 0] = xg_ref[i] + xg_ref[4 + i] * innovation
+def finish_kernel(ra_ref, rb_ref, up_ref, down_ref, sm_ref, we_ref, xg_ref, _, out_ref, held, sems):
+    odd = lax.axis_index("track") % 2 == 1
+    a = [ra_ref[n].astype(F32) for n in range(2)]
+    b = [rb_ref[n].astype(F32) for n in range(2)]
+    copies = []
+    for side in range(2):
+        edge = slice(128 * side, 128 * side + 128)
+        at = side * (W - 128)
+        cols = slice(at, at + 128)
+        place = picks(up_ref[0] if side else down_ref[0]).astype(BF16)
+        got = []
+        for n in range(2):
+            mine = jnp.where(odd, b[n], a[n]) if side else jnp.where(odd, a[n], b[n])
+            got.append(jnp.dot(place, mine.astype(BF16), preferred_element_type=F32))
+        weight = we_ref[:, edge] + WEIGHT_FLOOR
+        innovation = (weight * sm_ref[:, edge] + got[0]) / (weight + got[1])
+        for i in range(4):
+            held[side, i] = xg_ref[i, :, cols] + xg_ref[4 + i, :, cols] * innovation
+        copies.append(
+            pltpu.make_async_copy(held.at[side], out_ref.at[:, 0, :, pl.ds(at, 128)], sems.at[side])
+        )
+        copies[-1].start()
+    for copy in copies:
+        copy.wait()
 
 
 def finish(ra, rb, up, down, sm, we, xg, ns):
-    whole = lambda shape: pl.BlockSpec(shape, lambda i: (0,) * len(shape))
-    edge = pl.BlockSpec((R, 128), lambda i: (0, i))
     return pl.pallas_call(
         finish_kernel,
-        grid=(2,),
-        out_shape=jax.ShapeDtypeStruct(ns.shape, F32),
-        in_specs=[
-            whole((2, NB, 128)),
-            whole((2, NB, 128)),
-            whole((1, 1, NB)),
-            whole((1, 1, NB)),
-            edge,
-            edge,
-            pl.BlockSpec((8, R, 128), lambda i: (0, 0, 7 * i)),
-            ANY,
-        ],
-        out_specs=pl.BlockSpec((4, 1, R, 128), lambda i: (0, 0, 0, 7 * i)),
+        out_shape=pltpu.HBM(ns.shape, F32),
+        in_specs=[VMEM] * 7 + [ANY],
+        out_specs=ANY,
+        scratch_shapes=[pltpu.VMEM((2, 4, R, 128), F32), pltpu.SemaphoreType.DMA((2,))],
         input_output_aliases={7: 0},
         cost_estimate=pl.CostEstimate(flops=10**6, bytes_accessed=10**6, transcendentals=0),
         compiler_params=pltpu.CompilerParams(vmem_limit_bytes=3 * 2**20),

time: 41.8 us -> 40.7 us (0.974)
  Pallas kernels: 14.8 us -> 12.2 us
  waiting for transfers between devices: 0.36 us -> 1.95 us
    pallas_call x2, Pallas kernels: 4.1 us -> 2.38 us  [the longest x1 1.46 us: state(): pl.pallas_call(state_kernel, out_shape=pltpu.HBM((4, 1, R, W), F32), in_s...]
    all_to_all x1, waiting for transfers between devices: 0.35 us -> 1.15 us  [local(): part = lax.all_to_all(part, 'tile', split_axis=0, concat_axis=0, tiled=True)]
    pallas_call x1, Pallas kernels: 6.65 us -> 5.84 us  [covariance(): pl.pallas_call(cov_kernel, grid=(R // step,), out_shape=(jax.ShapeDtypeSt...]
    ppermute x4, waiting for transfers between devices: 0.01 us -> 0.8 us  [swap(): return lax.ppermute(value, axis, pairs)]
  transfers between devices with their start and end apart: 5 -> 5, of which waited for: 1 -> 2; matrix products, arithmetic and copies ran while one was open for 0% -> 0% of each run, Pallas kernels for 23% -> 18%
where the time goes in v4:
time: 40.7 us; the launch traced here: 40.5 us
  starting transfers between devices  25 us (61%)
  Pallas kernels  12.2 us (30%)
  waiting for transfers between devices  1.95 us (5%)
  between operations  1.35 us (3%)
    all_to_all x1, starting transfers between devices, local(): part = lax.all_to_all(part, 'tile', split_axis=0, concat_axis=0, tiled=True)  13.6 us
    ppermute x4, starting transfers between devices, swap(): return lax.ppermute(value, axis, pairs)  11.4 us
    pallas_call x1, Pallas kernels, covariance(): pl.pallas_call(cov_kernel, grid=(R // step,), out_shape=(jax.ShapeDtypeSt...  5.84 us
    pallas_call x1, Pallas kernels, front(): pl.pallas_call(functools.partial(front_kernel, tiles), out_shape=(pltpu.V...  3.5 us
    pallas_call x1, Pallas kernels, state(): pl.pallas_call(state_kernel, out_shape=pltpu.HBM((4, 1, R, W), F32), in_s...  1.46 us
    all_to_all x1, waiting for transfers between devices, local(): part = lax.all_to_all(part, 'tile', split_axis=0, concat_axis=0, tiled=True)  1.15 us
    pallas_call x1, Pallas kernels, finish(): pl.pallas_call(finish_kernel, out_shape=pltpu.HBM(ns.shape, F32), in_spec...  0.92 us
  transfers between devices with their start and end apart: 5, of which 2 were waited for; matrix products, arithmetic and copies ran while one was open for 0% of the time, Pallas kernels for 18%

profile of v4, /device:TPU:1, one launch (start us, length us, event | category | flops | bytes accessed | tf_op | source)
XLA Modules:
  0.0 40.5 jit_solution(6281046011273634337)
XLA Ops:
  0.6 0.0 copy-start.2
  1.3 3.5 %front.1 = (f32[96,1024]{1,0:T(8,128)S(1)}, bf16[64,24,128]{2,1,0:T(8,128)(2,1)}, f32[1,1024]{1,0:T(1,128)S(1)}, f32[1,1024]{1,0:T(1,128)S(1)}, f32[8,128]{1,0:T(8,128)S(1)}) custom-call(s32[1]{0:T(128)S(6)} %copy.19.scene_h, f32[16]{0:T(128)} %table_h.1, f32[1,80,1024]{2,1,0:T(8,128)} %d_ref.1, f32[1,80,1024]{2,1,0:T(8,128)} %v_ref.1, ...), custom_call_target="tpu_custom_call" | custom-call | flops 100000000 | bytes 4000000 | tf_op jit(solution)/shard_map/front/pallas_call | solution.py:175
  4.8 13.6 %all-to-all-start = ((bf16[64,24,128]{2,1,0:T(8,128)(2,1)}), bf16[64,24,128]{2,1,0:T(8,128)(2,1)S(1)}, u32[]{:S(2)}, u32[]{:S(2)}) async-start(bf16[64,24,128]{2,1,0:T(8,128)(2,1)} %get-tuple-element.14), calls=%async_computation | async-start | bytes 786432 | tf_op jit(solution)/shard_map/all_to_all | solution.py:483
  18.4 1.1 %collective-permute-start = (f32[1,1024]{1,0:T(1,128)S(1)}, f32[1,1024]{1,0:T(1,128)S(1)}, u32[]{:S(2)}, u32[]{:S(2)}) collective-permute-start(f32[1,1024]{1,0:T(1,128)S(1)} %get-tuple-element.16), channel_id=1, source_target_pairs={{0,1},{1,0},{2,3},{3,2},{4,5},{5,4},{6,7},{7,6},{8,9},{9,8},{10,11... | collective-permute-start | bytes 12296 | tf_op jit(solution)/shard_map/ppermute | solution.py:459
  19.5 4.8 %collective-permute-start.1 = (f32[1,1024]{1,0:T(1,128)S(1)}, f32[1,1024]{1,0:T(1,128)S(1)}, u32[]{:S(2)}, u32[]{:S(2)}) collective-permute-start(f32[1,1024]{1,0:T(1,128)S(1)} %get-tuple-element.17), channel_id=1, source_target_pairs={{1,2},{2,1},{3,4},{4,3},{5,6},{6,5},{7,8},{8,7},{9,10},{10,9},{11,... | collective-permute-start | bytes 12296 | tf_op jit(solution)/shard_map/ppermute | solution.py:459
  24.3 0.0 copy-done.2
  24.3 0.0 copy-start
  24.3 0.0 copy-start.1
  24.3 5.8 %covariance.1 = (f32[10,1,80,1024]{3,2,1,0:T(8,128)}, f32[8,80,1024]{2,1,0:T(8,128)S(1)}, f32[80,256]{1,0:T(8,128)S(1)}) custom-call(f32[8,128]{1,0:T(8,128)S(1)} %get-tuple-element.18.terms, f32[4]{0:T(128)S(1)} %copy-done.2, f32[1,80,1024]{2,1,0:T(8,128)} %d_ref.1, f32[1,80,1024]{2,1,0:T(8,128)} %v_ref.1, f32[2,1,80,1024]{3,2,1,0:T(8,128)} %s_ref.1, ...), custom_call_target="tpu_custom_call" | custom-call | flops 20000000 | bytes 12000000 | tf_op jit(solution)/shard_map/covariance/pallas_call | solution.py:274
  30.1 0.0 collective-permute-done.pa_ref
  30.2 0.0 collective-permute-done.1.pb_ref
  30.2 1.2 %all-to-all-done.part_ref = bf16[64,24,128]{2,1,0:T(8,128)(2,1)S(1)} async-done(((bf16[64,24,128]{2,1,0:T(8,128)(2,1)}), bf16[64,24,128]{2,1,0:T(8,128)(2,1)S(1)}, u32[]{:S(2)}, u32[]{:S(2)}) %all-to-all-start) | async-done | bytes 393248 | tf_op jit(solution)/shard_map/all_to_all | solution.py:483
  31.3 0.0 copy-done
  31.3 0.0 copy-done.1
  31.3 0.5 %margin.1 = (f32[24,128]{1,0:T(8,128)S(1)}, f32[80,256]{1,0:T(8,128)S(1)}, bf16[2,40,128]{2,1,0:T(8,128)(2,1)S(1)}, bf16[2,40,128]{2,1,0:T(8,128)(2,1)S(1)}) custom-call(bf16[64,24,128]{2,1,0:T(8,128)(2,1)S(1)} %all-to-all-done.part_ref, f32[96,1024]{1,0:T(8,128)S(1)} %get-tuple-element.15.raw_ref, f32[1,1024]{1,0:T(1,128)S(1)} %collective-permute-done.pa_ref, ...), custom_call_target="tpu_custom_call" | custom-call | flops 10000000 | bytes 1000000 | tf_op jit(solution)/shard_map/margin/pallas_call | solution.py:356
  31.8 3.1 %collective-permute-start.2 = (bf16[2,40,128]{2,1,0:T(8,128)(2,1)S(1)}, bf16[2,40,128]{2,1,0:T(8,128)(2,1)S(1)}, u32[]{:S(2)}, u32[]{:S(2)}) collective-permute-start(bf16[2,40,128]{2,1,0:T(8,128)(2,1)S(1)} %get-tuple-element.20), channel_id=1, source_target_pairs={{0,64},{64,0},{128,192},{192,128},{1,65},{65,1},{129,193},{193,129... | collective-permute-start | bytes 61448 | tf_op jit(solution)/shard_map/ppermute | solution.py:459
  34.8 2.4 %collective-permute-start.3 = (bf16[2,40,128]{2,1,0:T(8,128)(2,1)S(1)}, bf16[2,40,128]{2,1,0:T(8,128)(2,1)S(1)}, u32[]{:S(2)}, u32[]{:S(2)}) collective-permute-start(bf16[2,40,128]{2,1,0:T(8,128)(2,1)S(1)} %get-tuple-element.21), channel_id=1, source_target_pairs={{64,128},{128,64},{192,0},{0,192},{65,129},{129,65},{193,1},{1,193... | collective-permute-start | bytes 61448 | tf_op jit(solution)/shard_map/ppermute | solution.py:459
  37.3 1.5 %state.1._ = f32[4,1,80,1024]{3,2,1,0:T(8,128)} custom-call(f32[24,128]{1,0:T(8,128)S(1)} %get-tuple-element.24.screen_ref, f32[96,1024]{1,0:T(8,128)S(1)} %get-tuple-element.15.raw_ref, f32[1,1024]{1,0:T(1,128)S(1)} %collective-permute-done.pa_ref, f32[1,1024]{1,0:T(1,128)S(1)} %collective-permute-done.1.pb_ref, f32[8,80,1024]{2,1,0:T(8,128)S(1)} %get-tuple-element.23.xg_ref), custom_call_target="tpu_custom_call" | custom-call | flops 2000000 | bytes 4000000 | tf_op jit(solution)/shard_map/state/pallas_call | solution.py:397
  38.8 0.0 collective-permute-done.2.ra_ref
  38.8 0.8 %collective-permute-done.3.rb_ref = bf16[2,40,128]{2,1,0:T(8,128)(2,1)S(1)} collective-permute-done((bf16[2,40,128]{2,1,0:T(8,128)(2,1)S(1)}, bf16[2,40,128]{2,1,0:T(8,128)(2,1)S(1)}, u32[]{:S(2)}, u32[]{:S(2)}) %collective-permute-start.3) | collective-permute-done | bytes 20512 | tf_op jit(solution)/shard_map/ppermute | solution.py:459
  39.6 0.9 %finish.1 = f32[4,1,80,1024]{3,2,1,0:T(8,128)} custom-call(bf16[2,40,128]{2,1,0:T(8,128)(2,1)S(1)} %collective-permute-done.2.ra_ref, bf16[2,40,128]{2,1,0:T(8,128)(2,1)S(1)} %collective-permute-done.3.rb_ref, s32[1,1,40]{2,1,0:T(1,128)S(1)} %copy-done, s32[1,1,40]{2,1,0:T(1,128)S(1)} %copy-done.1, ...), custom_call_target="tpu_custom_call", output_to_operand_aliasing={{}: (7, {})} | custom-call | flops 1000000 | bytes 1000000 | tf_op jit(solution)/shard_map/finish/pallas_call | solution.py:440
Async XLA Ops:
  0.6 23.7 %copy-start.2 = (f32[4]{0:T(128)S(1)}, f32[4]{0:T(128)}, u32[]{:S(2)}) copy-start(f32[4]{0:T(128)} %noise.1) | copy-start | bytes 52
  4.8 26.5 %all-to-all-start = ((bf16[64,24,128]{2,1,0:T(8,128)(2,1)}), bf16[64,24,128]{2,1,0:T(8,128)(2,1)S(1)}, u32[]{:S(2)}, u32[]{:S(2)}) async-start(bf16[64,24,128]{2,1,0:T(8,128)(2,1)} %get-tuple-element.14), calls=%async_computation | async-start | bytes 786432 | tf_op jit(solution)/shard_map/all_to_all | solution.py:483
  18.4 11.8 %collective-permute-start = (f32[1,1024]{1,0:T(1,128)S(1)}, f32[1,1024]{1,0:T(1,128)S(1)}, u32[]{:S(2)}, u32[]{:S(2)}) collective-permute-start(f32[1,1024]{1,0:T(1,128)S(1)} %get-tuple-element.16), channel_id=1, source_target_pairs={{0,1},{1,0},{2,3},{3,2},{4,5},{5,4},{6,7},{7,6},{8,9},{9,8},{10,11... | collective-permute-start | bytes 12296 | tf_op jit(solution)/shard_map/ppermute | solution.py:459
  19.5 10.7 %collective-permute-start.1 = (f32[1,1024]{1,0:T(1,128)S(1)}, f32[1,1024]{1,0:T(1,128)S(1)}, u32[]{:S(2)}, u32[]{:S(2)}) collective-permute-start(f32[1,1024]{1,0:T(1,128)S(1)} %get-tuple-element.17), channel_id=1, source_target_pairs={{1,2},{2,1},{3,4},{4,3},{5,6},{6,5},{7,8},{8,7},{9,10},{10,9},{11,... | collective-permute-start | bytes 12296 | tf_op jit(solution)/shard_map/ppermute | solution.py:459
  24.3 7.0 %copy-start = (s32[1,1,40]{2,1,0:T(1,128)S(1)}, s32[1,1,40]{2,1,0:T(1,128)}, u32[]{:S(2)}) copy-start(s32[1,1,40]{2,1,0:T(1,128)} %up_ref.3) | copy-start | bytes 484
  24.3 7.0 %copy-start.1 = (s32[1,1,40]{2,1,0:T(1,128)S(1)}, s32[1,1,40]{2,1,0:T(1,128)}, u32[]{:S(2)}) copy-start(s32[1,1,40]{2,1,0:T(1,128)} %down_ref.3) | copy-start | bytes 484
  31.8 7.0 %collective-permute-start.2 = (bf16[2,40,128]{2,1,0:T(8,128)(2,1)S(1)}, bf16[2,40,128]{2,1,0:T(8,128)(2,1)S(1)}, u32[]{:S(2)}, u32[]{:S(2)}) collective-permute-start(bf16[2,40,128]{2,1,0:T(8,128)(2,1)S(1)} %get-tuple-element.20), channel_id=1, source_target_pairs={{0,64},{64,0},{128,192},{192,128},{1,65},{65,1},{129,193},{193,129... | collective-permute-start | bytes 61448 | tf_op jit(solution)/shard_map/ppermute | solution.py:459
  34.8 4.7 %collective-permute-start.3 = (bf16[2,40,128]{2,1,0:T(8,128)(2,1)S(1)}, bf16[2,40,128]{2,1,0:T(8,128)(2,1)S(1)}, u32[]{:S(2)}, u32[]{:S(2)}) collective-permute-start(bf16[2,40,128]{2,1,0:T(8,128)(2,1)S(1)} %get-tuple-element.21), channel_id=1, source_target_pairs={{64,128},{128,64},{192,0},{0,192},{65,129},{129,65},{193,1},{1,193... | collective-permute-start | bytes 61448 | tf_op jit(solution)/shard_map/ppermute | solution.py:459

commit v5 on v4

--- a/solution.py
+++ b/solution.py
@@ -291,10 +291,10 @@
     )(vmem(terms), noise, *map(hbm, (d, v, s, cd, cc, nv, co, va)))
 
 
-def clean_window(cl, screen, raw_ref, pa_ref, pb_ref, blocks):
+def clean_window(cl, screen, raw_ref, pa_ref, pb_ref, blocks, groups=range(4)):
     odd = lax.axis_index("tile") % 2 == 1
     lane = lax.broadcasted_iota(jnp.int32, (SUB, 128), 1) // 32
-    for g in range(4):
+    for g in groups:
         rows = slice(g * SUB, (g + 1) * SUB)
         for n, b in enumerate(blocks):
             spread = jnp.take_along_axis(screen, lane + (32 * g + 4 * b), axis=1)
@@ -304,8 +304,10 @@
     for n, b in enumerate(blocks):
         c = slice(128 * n, 128 * (n + 1))
         o = slice(128 * b, 128 * (b + 1))
-        cl[PAD - 1 : PAD, c] = cl[PAD - 1 : PAD, c] + above[:, o]
-        cl[PAD + R : PAD + R + 1, c] = cl[PAD + R : PAD + R + 1, c] + below[:, o]
+        if 0 in groups:
+            cl[PAD - 1 : PAD, c] = cl[PAD - 1 : PAD, c] + above[:, o]
+        if 3 in groups:
+            cl[PAD + R : PAD + R + 1, c] = cl[PAD + R : PAD + R + 1, c] + below[:, o]
 
 
 def smoothed(up, mid, down):
@@ -371,11 +373,16 @@
 
 
 def state_kernel(screen_ref, raw_ref, pa_ref, pb_ref, xg_ref, out_ref, cl, held, sems):
-    clean_window(cl, screen_ref[...], raw_ref, pa_ref, pb_ref, tuple(range(8)))
+    screen = screen_ref[...]
     step = R // 5
-    copies = []
+    copies, cleaned = [], 0
     for n in range(5):
         r0 = n * step
+        needed = min(4, (PAD + r0 + step) // SUB + 1)
+        if needed > cleaned:
+            groups = range(cleaned, needed)
+            clean_window(cl, screen, raw_ref, pa_ref, pb_ref, tuple(range(8)), groups)
+            cleaned = needed
         rows = slice(r0, r0 + step)
         smooth = smoothed(
             cl[PAD - 1 + r0 : PAD - 1 + r0 + step],

time: 40.7 us -> 40.7 us (level)
  no operation moved by 1% of the time
where the time goes in v5:
time: 40.7 us; the launch traced here: 40.5 us
  starting transfers between devices  25 us (61%)
  Pallas kernels  12.1 us (30%)
  waiting for transfers between devices  2.04 us (5%)
  between operations  1.35 us (3%)
    all_to_all x1, starting transfers between devices, local(): part = lax.all_to_all(part, 'tile', split_axis=0, concat_axis=0, tiled=True)  13.6 us
    ppermute x4, starting transfers between devices, swap(): return lax.ppermute(value, axis, pairs)  11.4 us
    pallas_call x1, Pallas kernels, covariance(): pl.pallas_call(cov_kernel, grid=(R // step,), out_shape=(jax.ShapeDtypeSt...  5.84 us
    pallas_call x1, Pallas kernels, front(): pl.pallas_call(functools.partial(front_kernel, tiles), out_shape=(pltpu.V...  3.5 us
    pallas_call x1, Pallas kernels, state(): pl.pallas_call(state_kernel, out_shape=pltpu.HBM((4, 1, R, W), F32), in_s...  1.37 us
    all_to_all x1, waiting for transfers between devices, local(): part = lax.all_to_all(part, 'tile', split_axis=0, concat_axis=0, tiled=True)  1.15 us
    pallas_call x1, Pallas kernels, finish(): pl.pallas_call(finish_kernel, out_shape=pltpu.HBM(ns.shape, F32), in_spec...  0.92 us
    ppermute x4, waiting for transfers between devices, swap(): return lax.ppermute(value, axis, pairs)  0.89 us
  transfers between devices with their start and end apart: 5, of which 2 were waited for; matrix products, arithmetic and copies ran while one was open for 0% of the time, Pallas kernels for 18%

profile of v5, /device:TPU:1, one launch (start us, length us, event | category | flops | bytes accessed | tf_op | source)
XLA Modules:
  0.0 40.5 jit_solution(1094886255113640614)
XLA Ops:
  0.6 0.0 copy-start.2
  1.3 3.5 %front.1 = (f32[96,1024]{1,0:T(8,128)S(1)}, bf16[64,24,128]{2,1,0:T(8,128)(2,1)}, f32[1,1024]{1,0:T(1,128)S(1)}, f32[1,1024]{1,0:T(1,128)S(1)}, f32[8,128]{1,0:T(8,128)S(1)}) custom-call(s32[1]{0:T(128)S(6)} %copy.19.scene_h, f32[16]{0:T(128)} %table_h.1, f32[1,80,1024]{2,1,0:T(8,128)} %d_ref.1, f32[1,80,1024]{2,1,0:T(8,128)} %v_ref.1, ...), custom_call_target="tpu_custom_call" | custom-call | flops 100000000 | bytes 4000000 | tf_op jit(solution)/shard_map/front/pallas_call | solution.py:175
  4.8 13.6 %all-to-all-start = ((bf16[64,24,128]{2,1,0:T(8,128)(2,1)}), bf16[64,24,128]{2,1,0:T(8,128)(2,1)S(1)}, u32[]{:S(2)}, u32[]{:S(2)}) async-start(bf16[64,24,128]{2,1,0:T(8,128)(2,1)} %get-tuple-element.14), calls=%async_computation | async-start | bytes 786432 | tf_op jit(solution)/shard_map/all_to_all | solution.py:490
  18.4 1.1 %collective-permute-start = (f32[1,1024]{1,0:T(1,128)S(1)}, f32[1,1024]{1,0:T(1,128)S(1)}, u32[]{:S(2)}, u32[]{:S(2)}) collective-permute-start(f32[1,1024]{1,0:T(1,128)S(1)} %get-tuple-element.16), channel_id=1, source_target_pairs={{0,1},{1,0},{2,3},{3,2},{4,5},{5,4},{6,7},{7,6},{8,9},{9,8},{10,11... | collective-permute-start | bytes 12296 | tf_op jit(solution)/shard_map/ppermute | solution.py:466
  19.5 4.8 %collective-permute-start.1 = (f32[1,1024]{1,0:T(1,128)S(1)}, f32[1,1024]{1,0:T(1,128)S(1)}, u32[]{:S(2)}, u32[]{:S(2)}) collective-permute-start(f32[1,1024]{1,0:T(1,128)S(1)} %get-tuple-element.17), channel_id=1, source_target_pairs={{1,2},{2,1},{3,4},{4,3},{5,6},{6,5},{7,8},{8,7},{9,10},{10,9},{11,... | collective-permute-start | bytes 12296 | tf_op jit(solution)/shard_map/ppermute | solution.py:466
  24.3 0.0 copy-done.2
  24.3 0.0 copy-start
  24.3 0.0 copy-start.1
  24.3 5.8 %covariance.1 = (f32[10,1,80,1024]{3,2,1,0:T(8,128)}, f32[8,80,1024]{2,1,0:T(8,128)S(1)}, f32[80,256]{1,0:T(8,128)S(1)}) custom-call(f32[8,128]{1,0:T(8,128)S(1)} %get-tuple-element.18.terms, f32[4]{0:T(128)S(1)} %copy-done.2, f32[1,80,1024]{2,1,0:T(8,128)} %d_ref.1, f32[1,80,1024]{2,1,0:T(8,128)} %v_ref.1, f32[2,1,80,1024]{3,2,1,0:T(8,128)} %s_ref.1, ...), custom_call_target="tpu_custom_call" | custom-call | flops 20000000 | bytes 12000000 | tf_op jit(solution)/shard_map/covariance/pallas_call | solution.py:274
  30.1 0.0 collective-permute-done.pa_ref
  30.2 0.0 collective-permute-done.1.pb_ref
  30.2 1.2 %all-to-all-done.part_ref = bf16[64,24,128]{2,1,0:T(8,128)(2,1)S(1)} async-done(((bf16[64,24,128]{2,1,0:T(8,128)(2,1)}), bf16[64,24,128]{2,1,0:T(8,128)(2,1)S(1)}, u32[]{:S(2)}, u32[]{:S(2)}) %all-to-all-start) | async-done | bytes 393248 | tf_op jit(solution)/shard_map/all_to_all | solution.py:490
  31.3 0.0 copy-done
  31.3 0.0 copy-done.1
  31.3 0.5 %margin.1 = (f32[24,128]{1,0:T(8,128)S(1)}, f32[80,256]{1,0:T(8,128)S(1)}, bf16[2,40,128]{2,1,0:T(8,128)(2,1)S(1)}, bf16[2,40,128]{2,1,0:T(8,128)(2,1)S(1)}) custom-call(bf16[64,24,128]{2,1,0:T(8,128)(2,1)S(1)} %all-to-all-done.part_ref, f32[96,1024]{1,0:T(8,128)S(1)} %get-tuple-element.15.raw_ref, f32[1,1024]{1,0:T(1,128)S(1)} %collective-permute-done.pa_ref, ...), custom_call_target="tpu_custom_call" | custom-call | flops 10000000 | bytes 1000000 | tf_op jit(solution)/shard_map/margin/pallas_call | solution.py:358
  31.8 3.1 %collective-permute-start.2 = (bf16[2,40,128]{2,1,0:T(8,128)(2,1)S(1)}, bf16[2,40,128]{2,1,0:T(8,128)(2,1)S(1)}, u32[]{:S(2)}, u32[]{:S(2)}) collective-permute-start(bf16[2,40,128]{2,1,0:T(8,128)(2,1)S(1)} %get-tuple-element.20), channel_id=1, source_target_pairs={{0,64},{64,0},{128,192},{192,128},{1,65},{65,1},{129,193},{193,129... | collective-permute-start | bytes 61448 | tf_op jit(solution)/shard_map/ppermute | solution.py:466
  34.8 2.4 %collective-permute-start.3 = (bf16[2,40,128]{2,1,0:T(8,128)(2,1)S(1)}, bf16[2,40,128]{2,1,0:T(8,128)(2,1)S(1)}, u32[]{:S(2)}, u32[]{:S(2)}) collective-permute-start(bf16[2,40,128]{2,1,0:T(8,128)(2,1)S(1)} %get-tuple-element.21), channel_id=1, source_target_pairs={{64,128},{128,64},{192,0},{0,192},{65,129},{129,65},{193,1},{1,193... | collective-permute-start | bytes 61448 | tf_op jit(solution)/shard_map/ppermute | solution.py:466
  37.3 1.4 %state.1._ = f32[4,1,80,1024]{3,2,1,0:T(8,128)} custom-call(f32[24,128]{1,0:T(8,128)S(1)} %get-tuple-element.24.screen_ref, f32[96,1024]{1,0:T(8,128)S(1)} %get-tuple-element.15.raw_ref, f32[1,1024]{1,0:T(1,128)S(1)} %collective-permute-done.pa_ref, f32[1,1024]{1,0:T(1,128)S(1)} %collective-permute-done.1.pb_ref, f32[8,80,1024]{2,1,0:T(8,128)S(1)} %get-tuple-element.23.xg_ref), custom_call_target="tpu_custom_call" | custom-call | flops 2000000 | bytes 4000000 | tf_op jit(solution)/shard_map/state/pallas_call | solution.py:404
  38.7 0.0 collective-permute-done.2.ra_ref
  38.7 0.9 %collective-permute-done.3.rb_ref = bf16[2,40,128]{2,1,0:T(8,128)(2,1)S(1)} collective-permute-done((bf16[2,40,128]{2,1,0:T(8,128)(2,1)S(1)}, bf16[2,40,128]{2,1,0:T(8,128)(2,1)S(1)}, u32[]{:S(2)}, u32[]{:S(2)}) %collective-permute-start.3) | collective-permute-done | bytes 20512 | tf_op jit(solution)/shard_map/ppermute | solution.py:466
  39.6 0.9 %finish.1 = f32[4,1,80,1024]{3,2,1,0:T(8,128)} custom-call(bf16[2,40,128]{2,1,0:T(8,128)(2,1)S(1)} %collective-permute-done.2.ra_ref, bf16[2,40,128]{2,1,0:T(8,128)(2,1)S(1)} %collective-permute-done.3.rb_ref, s32[1,1,40]{2,1,0:T(1,128)S(1)} %copy-done, s32[1,1,40]{2,1,0:T(1,128)S(1)} %copy-done.1, ...), custom_call_target="tpu_custom_call", output_to_operand_aliasing={{}: (7, {})} | custom-call | flops 1000000 | bytes 1000000 | tf_op jit(solution)/shard_map/finish/pallas_call | solution.py:447
Async XLA Ops:
  0.6 23.7 %copy-start.2 = (f32[4]{0:T(128)S(1)}, f32[4]{0:T(128)}, u32[]{:S(2)}) copy-start(f32[4]{0:T(128)} %noise.1) | copy-start | bytes 52
  4.8 26.5 %all-to-all-start = ((bf16[64,24,128]{2,1,0:T(8,128)(2,1)}), bf16[64,24,128]{2,1,0:T(8,128)(2,1)S(1)}, u32[]{:S(2)}, u32[]{:S(2)}) async-start(bf16[64,24,128]{2,1,0:T(8,128)(2,1)} %get-tuple-element.14), calls=%async_computation | async-start | bytes 786432 | tf_op jit(solution)/shard_map/all_to_all | solution.py:490
  18.4 11.8 %collective-permute-start = (f32[1,1024]{1,0:T(1,128)S(1)}, f32[1,1024]{1,0:T(1,128)S(1)}, u32[]{:S(2)}, u32[]{:S(2)}) collective-permute-start(f32[1,1024]{1,0:T(1,128)S(1)} %get-tuple-element.16), channel_id=1, source_target_pairs={{0,1},{1,0},{2,3},{3,2},{4,5},{5,4},{6,7},{7,6},{8,9},{9,8},{10,11... | collective-permute-start | bytes 12296 | tf_op jit(solution)/shard_map/ppermute | solution.py:466
  19.5 10.7 %collective-permute-start.1 = (f32[1,1024]{1,0:T(1,128)S(1)}, f32[1,1024]{1,0:T(1,128)S(1)}, u32[]{:S(2)}, u32[]{:S(2)}) collective-permute-start(f32[1,1024]{1,0:T(1,128)S(1)} %get-tuple-element.17), channel_id=1, source_target_pairs={{1,2},{2,1},{3,4},{4,3},{5,6},{6,5},{7,8},{8,7},{9,10},{10,9},{11,... | collective-permute-start | bytes 12296 | tf_op jit(solution)/shard_map/ppermute | solution.py:466
  24.3 7.0 %copy-start = (s32[1,1,40]{2,1,0:T(1,128)S(1)}, s32[1,1,40]{2,1,0:T(1,128)}, u32[]{:S(2)}) copy-start(s32[1,1,40]{2,1,0:T(1,128)} %up_ref.3) | copy-start | bytes 484
  24.3 7.0 %copy-start.1 = (s32[1,1,40]{2,1,0:T(1,128)S(1)}, s32[1,1,40]{2,1,0:T(1,128)}, u32[]{:S(2)}) copy-start(s32[1,1,40]{2,1,0:T(1,128)} %down_ref.3) | copy-start | bytes 484
  31.8 6.9 %collective-permute-start.2 = (bf16[2,40,128]{2,1,0:T(8,128)(2,1)S(1)}, bf16[2,40,128]{2,1,0:T(8,128)(2,1)S(1)}, u32[]{:S(2)}, u32[]{:S(2)}) collective-permute-start(bf16[2,40,128]{2,1,0:T(8,128)(2,1)S(1)} %get-tuple-element.20), channel_id=1, source_target_pairs={{0,64},{64,0},{128,192},{192,128},{1,65},{65,1},{129,193},{193,129... | collective-permute-start | bytes 61448 | tf_op jit(solution)/shard_map/ppermute | solution.py:466
  34.8 4.7 %collective-permute-start.3 = (bf16[2,40,128]{2,1,0:T(8,128)(2,1)S(1)}, bf16[2,40,128]{2,1,0:T(8,128)(2,1)S(1)}, u32[]{:S(2)}, u32[]{:S(2)}) collective-permute-start(bf16[2,40,128]{2,1,0:T(8,128)(2,1)S(1)} %get-tuple-element.21), channel_id=1, source_target_pairs={{64,128},{128,64},{192,0},{0,192},{65,129},{129,65},{193,1},{1,193... | collective-permute-start | bytes 61448 | tf_op jit(solution)/shard_map/ppermute | solution.py:466
